TPU v7x, 32 devices: a whole 2x2x4 slice. The times are simulated.
32 devices in a mesh: group: 16 (over z, y, core), shard: 2 (over x).
Axes of the slice: x: 2, y: 2, z: 4, core: 2. Of those that a mesh axis runs over, the one named last changes fastest.
Arguments:
- frames: bfloat16 [64, 256, 512], P(('group', 'shard')), may hold values from -6 to 6
- lengths: int32 [64], P(('group', 'shard')), may hold values from 128 to 256, as said below
- cotangent: bfloat16 [64, 256, 512], P(('group', 'shard')), may hold values from -6 to 6
- ffn_in: float32 [2, 512, 2048], P(None, 'shard'), may hold values from -0.25 to 0.25
- ffn_in_moment: float32 [2, 512, 2048], P(None, 'shard'), may hold values from -10 to 10
- ffn_in_square: float32 [2, 512, 2048], P(None, 'shard'), may hold values from 0.2768896 to 1.1075584
- ffn_out: float32 [2, 2048, 512], P(None, 'shard'), may hold values from -0.25 to 0.25
- ffn_out_moment: float32 [2, 2048, 512], P(None, 'shard'), may hold values from -10 to 10
- ffn_out_square: float32 [2, 2048, 512], P(None, 'shard'), may hold values from 0.2768896 to 1.1075584
- attn_proj: float32 [4, 512, 512], P(None, 'shard')
- attn_moment: float32 [4, 512, 512], P(None, 'shard')
- attn_square: float32 [4, 512, 512], P(None, 'shard')
- conv_proj: float32 [512, 1536], P('shard')
- conv_moment: float32 [512, 1536], P('shard'), may hold values from -32 to 32
- conv_square: float32 [512, 1536], P('shard'), may hold values from 2.62144 to 10.48576
- vectors: float32 [37, 512], P(None, 'shard')
- vectors_moment: float32 [37, 512], P(None, 'shard'), may hold values from -32 to 32
- vectors_square: float32 [37, 512], P(None, 'shard'), may hold values from 2.62144 to 10.48576
- rel_keys: float32 [73, 64], replicated, may hold values from -4 to 4
- rel_moment: float32 [73, 64], replicated, may hold values from -40 to 40
- rel_square: float32 [73, 64], replicated, may hold values from 4.096 to 16.384
Outputs:
- output: bfloat16 [64, 256, 512], P(('group', 'shard'))
- input_grad: bfloat16 [64, 256, 512], P(('group', 'shard'))
- grad_ffn_in: float32 [2, 512, 2048], P(None, 'shard')
- new_ffn_in: float32 [2, 512, 2048], P(None, 'shard')
- new_ffn_in_moment: float32 [2, 512, 2048], P(None, 'shard')
- new_ffn_in_square: float32 [2, 512, 2048], P(None, 'shard')
- grad_ffn_out: float32 [2, 2048, 512], P(None, 'shard')
- new_ffn_out: float32 [2, 2048, 512], P(None, 'shard')
- new_ffn_out_moment: float32 [2, 2048, 512], P(None, 'shard')
- new_ffn_out_square: float32 [2, 2048, 512], P(None, 'shard')
- grad_attn_proj: float32 [4, 512, 512], P(None, 'shard')
- new_attn_proj: float32 [4, 512, 512], P(None, 'shard')
- new_attn_moment: float32 [4, 512, 512], P(None, 'shard')
- new_attn_square: float32 [3, 512, 512], P(None, 'shard')
- new_attn_out_square: float32 [512, 512], P('shard')
- grad_conv_proj: float32 [512, 1536], P('shard')
- new_conv_proj: float32 [512, 1536], P('shard')
- new_conv_moment: float32 [512, 1536], P('shard')
- new_conv_square: float32 [512, 1536], P('shard')
- grad_vectors: float32 [37, 512], P(None, 'shard')
- new_vectors: float32 [37, 512], P(None, 'shard')
- new_vectors_moment: float32 [37, 512], P(None, 'shard')
- new_vectors_square: float32 [37, 512], P(None, 'shard')
- grad_rel_keys: float32 [73, 64], replicated
- new_rel_keys: float32 [73, 64], replicated
- new_rel_moment: float32 [73, 64], replicated
- new_rel_square: float32 [73, 64], replicated
- trust_norms: float32 [2, 18], replicated
Inputs may be any that keep to these rules, and one draw needn't show every extreme that they name: `lengths`: every sequence has at least 128 valid frames; the first sequence has all 256.
All inputs are finite; a program needn't handle non-finite values.
Results may differ from a plain program's by a relative error of at most 0.02.
Values may be sent and summed in bfloat16 or wider, within the bound.
No kernel may reach another device: no remote copies, remote signals or barrier semaphores. Data moves between devices by JAX's collectives and lax.ppermute only.
A program may use at most 320 MiB of HBM per device.

v0:
```python
import math

import jax
import jax.numpy as jnp
from jax import lax
from jax.experimental import pallas as pl
from jax.experimental.pallas import tpu as pltpu
from jax.sharding import PartitionSpec as P

D = 512
FF = 2048
HEADS = 8
HEAD = 64
KERNEL = 31
BACK = 64
AHEAD = 8
RELS = 73
STEP = 10
PIECES = 32
LEAD = 32
FFN_ROWS = 128
ATTN_ROWS = 64
CONV_ROWS = 48

NORM_EPSILON = 1e-05
ADAM_EPSILON = 1e-06
RATIO_EPSILON = 1e-06
BETA_FIRST = 0.9
BETA_SECOND = 0.999
WEIGHT_DECAY = 0.01
LEARN_RATE = 0.5
MASKED_SCORE = -1e30

bf16 = jnp.bfloat16
f32 = jnp.float32
VMEM_LIMIT = 24 * 1024 * 1024
STREAM_LIMIT = 60 * 1024 * 1024


def vmem():
    return pl.BlockSpec(memory_space=pltpu.VMEM)


def smem():
    return pl.BlockSpec(memory_space=pltpu.SMEM)


def shape(dims, kind):
    return jax.ShapeDtypeStruct(dims, kind)


def dot(left, right):
    return jnp.dot(left, right, preferred_element_type=f32)


def dot_rows(left, right):
    return lax.dot_general(left, right, (((0,), (0,)), ((), ())), preferred_element_type=f32)


def dot_cols(left, right):
    return lax.dot_general(left, right, (((1,), (1,)), ((), ())), preferred_element_type=f32)


def stats(values):
    centred = values - jnp.mean(values, axis=-1, keepdims=True)
    scale = lax.rsqrt(jnp.mean(centred * centred, axis=-1, keepdims=True) + NORM_EPSILON)
    return centred * scale, scale


def norm_back(grad, normed, scale, gain):
    grad_gain = jnp.sum(grad * normed, axis=0, keepdims=True)
    scaled = grad * gain
    inner = jnp.mean(scaled * normed, axis=-1, keepdims=True)
    back = scale * (scaled - jnp.mean(scaled, axis=-1, keepdims=True) - normed * inner)
    return back, grad_gain


def logistic(values):
    return 1.0 / (1.0 + jnp.exp(-values))


def slope_of(values, sig):
    return sig * (1.0 + values * (1.0 - sig))


class Plan:
    def __init__(self, groups, shards):
        self.groups, self.shards = groups, shards
        shard_bits = shards.bit_length() - 1
        group_bits = groups.bit_length() - 1
        self.used = min(5 - shard_bits, group_bits)
        self.owned = PIECES // shards
        order = [("group", 0)] + [("shard", b) for b in range(shard_bits)]
        order += [("group", b) for b in range(1, self.used)]
        self.order = order
        self.rest = [("group", b) for b in range(self.used, group_bits)]
        self.shard_bits = [("shard", b) for b in range(shard_bits)]
        self.kept = [step for step in order if step[0] == "group"]

    def piece_bit(self, step):
        return step[1] if step[0] == "group" else self.used + step[1]

    def place(self, piece):
        out = 0
        for step in self.order:
            out = out * 2 + ((piece >> self.piece_bit(step)) & 1)
        return out

    def kept_place(self, piece):
        out = 0
        for step in self.kept:
            out = out * 2 + ((piece >> step[1]) & 1)
        return out


def swap(values, step):
    axis, bit = step
    count = lax.axis_size(axis)
    return lax.ppermute(values, axis, [(i, i ^ (1 << bit)) for i in range(count)])


def add_low(left, right):
    return (left.astype(f32) + right.astype(f32)).astype(bf16)


class Chain:
    def __init__(self, kept, sent, plan):
        order, back = list(plan.order), list(reversed(plan.kept))
        self.todo = [("halve", step) for step in order]
        self.todo += [("add", step) for step in plan.rest] + [("keep", step) for step in back]
        self.kept, self.sent = kept, (sent,)

    def start(self):
        if self.todo:
            self.found = swap(self.sent[0], self.todo[0][1])

    def finish(self):
        if not self.todo:
            return
        kind, _ = self.todo.pop(0)
        coming = self.todo[0][0] if self.todo else None
        if kind == "keep":
            if coming is None:
                self.kept = (self.kept, self.found)
            else:
                self.kept = jnp.concatenate([self.kept, self.found], axis=0)
                self.sent = (self.kept,)
        elif coming == "halve":
            half = self.kept.shape[0] // 2
            low = add_low(self.kept[:half], self.found[:half])
            self.sent = (add_low(self.kept[half:], self.found[half:]),)
            self.kept = low
        else:
            self.kept = add_low(self.kept, self.found)
            self.sent = (self.kept,)


def merged(one, two, plan):
    both = Chain(
        jnp.concatenate([one.kept, two.kept], axis=1),
        jnp.concatenate([one.sent[0], two.sent[0]], axis=1),
        plan,
    )
    both.todo = list(one.todo)
    return both


class Everywhere:
    def __init__(self, values, plan):
        self.todo = plan.order + plan.rest
        self.kept, self.sent = values, (values,)

    def start(self):
        if self.todo:
            self.found = swap(self.sent[0], self.todo[0])

    def finish(self):
        if self.todo:
            self.todo = self.todo[1:]
            self.kept = self.kept + self.found
            self.sent = (self.kept,)


def gate(values, signs):
    held = lax.optimization_barrier((tuple(values), tuple(signs)))
    return held[0]


def beside(chains, run, first, sign):
    chains = [chain for chain in chains if chain.todo]
    first = gate(first, [v for chain in chains for v in chain.sent])
    for chain in chains:
        chain.start()
    outs = run(*first)
    for chain, value in zip(chains, gate([chain.kept for chain in chains], [outs[sign]])):
        chain.kept = value
    for chain in chains:
        chain.finish()
    return outs


def advance(chains, rounds):
    for _ in range(rounds):
        busy = [chain for chain in chains if chain.todo]
        for chain, value in zip(busy, gate([chain.sent for chain in busy], [])):
            chain.sent = tuple(value)
        for chain in busy:
            chain.start()
        for chain in busy:
            chain.finish()


def sum_shards(values, plan):
    for step in plan.shard_bits:
        values = values + swap(values, step)
    return values


def rounded_halves(plan, core, *owns):
    if plan.shards != 2:
        return [None] * len(owns)
    ins, specs, outs, out_specs = [], [], [], []
    for own, dim, layer in owns:
        dims = list(own.shape)
        dims[dim] //= 2
        if layer is not None:
            dims[0] = 1
        axes = len(dims)
        ins.append(own)

        def at(i, core_ref, axes=axes, dim=dim, layer=layer):
            return tuple(core_ref[0] if d == dim else (layer or 0) if d == 0 else 0 for d in range(axes))

        specs.append(pl.BlockSpec(tuple(dims), at))
        outs.append(shape(tuple(dims), bf16))
        out_specs.append(pl.BlockSpec(tuple(dims), lambda i, core_ref, axes=axes: (0,) * axes))

    def kernel(core_ref, *refs):
        for k in range(len(owns)):
            refs[len(owns) + k][...] = refs[k][...].astype(bf16)

    found = pl.pallas_call(
        kernel,
        out_shape=outs,
        grid_spec=pltpu.PrefetchScalarGridSpec(
            num_scalar_prefetch=1, grid=(1,), in_specs=specs, out_specs=out_specs
        ),
        compiler_params=pltpu.CompilerParams(vmem_limit_bytes=STREAM_LIMIT),
        name="rounded_halves",
    )(core.reshape(1).astype(jnp.int32), *ins)
    return [v if layer is None else v[0] for v, (_, _, layer) in zip(found, owns)]


def rounded_rows(plan, core, ffn_in, ffn_out, attn_proj, conv_proj):
    if plan.shards != 2:
        return [None] * 6, [None] * 4
    owns = [(ffn_in, 0), (ffn_out, 0), (ffn_in, 1), (ffn_out, 1)]
    outs = [shape(w.shape[1:], bf16) for w, _ in owns] + [shape(attn_proj.shape, bf16), shape(conv_proj.shape, bf16)]
    halved = [outs[4], outs[5], outs[2], outs[3]]
    for v in halved:
        dims = list(v.shape)
        dims[-2] //= 2
        outs.append(shape(tuple(dims), bf16))

    def kernel(core_ref, in_ref, out_ref, attn_ref, conv_ref, *refs):
        rows = refs[:6]
        for layer in range(2):
            rows[2 * layer][...] = in_ref[layer].astype(bf16)
            rows[2 * layer + 1][...] = out_ref[layer].astype(bf16)
        rows[4][...] = attn_ref[...].astype(bf16)
        rows[5][...] = conv_ref[...].astype(bf16)
        for source, half_ref in zip((rows[4], rows[5], rows[2], rows[3]), refs[6:]):
            half = half_ref.shape[-2]
            span = pl.ds(pl.multiple_of(core_ref[0] * half, half), half)
            half_ref[...] = source[:, span, :] if len(half_ref.shape) == 3 else source[span, :]

    found = call(
        kernel,
        outs,
        [core.reshape(1).astype(jnp.int32), ffn_in, ffn_out, attn_proj, conv_proj],
        [smem()] + [vmem()] * 4,
        (),
        "rounded_rows",
    )
    return found[:6], found[6:]


class Fetch:
    def __init__(self, own, dim, plan, rows, half, layer=None):
        self.own, self.plan, self.dim = rows, plan, dim
        if plan.shards == 2:
            self.value = half
        else:
            one = own if layer is None else own[layer]
            self.value = lax.all_gather(one.astype(bf16), "shard", axis=dim, tiled=True)

    def near(self):
        if self.plan.shards == 2:
            self.value = swap(self.value, ("shard", 0))

    def far(self):
        if self.plan.shards == 2:
            return (self.own, self.value, swap(self.value, ("group", 0)))
        return (self.value,)


def order(later, signs):
    for fetch, value in zip(later, gate([f.value for f in later], signs)):
        fetch.value = value


def join(place_ref, part_refs, whole_ref):
    if len(part_refs) == 1:
        whole_ref[...] = part_refs[0][...]
        return
    own, near, far = part_refs
    rows = own.shape[-2]
    half = rows // 2
    shard, core = place_ref[0], place_ref[1]
    first = pl.multiple_of(shard * rows, half)
    second = pl.multiple_of((1 - shard) * rows + core * half, half)
    third = pl.multiple_of((1 - shard) * rows + (1 - core) * half, half)
    if len(own.shape) == 2:
        whole_ref[pl.ds(second, half), :] = near[...]
        whole_ref[pl.ds(third, half), :] = far[...]
        whole_ref[pl.ds(first, rows), :] = own[...]
    else:
        for k in range(own.shape[0]):
            whole_ref[k, pl.ds(first, rows), :] = own[k]
            whole_ref[k, pl.ds(second, half), :] = near[k]
            whole_ref[k, pl.ds(third, half), :] = far[k]


def put(out_refs, plan, place_ref, value, row, rows_each, first):
    kept_ref, sent_ref = out_refs
    low = value.astype(bf16)
    core, mine = place_ref[1] == 0, place_ref[2]
    for k in range(0, value.shape[0] // rows_each, 2):
        even = low[k * rows_each : (k + 1) * rows_each]
        odd = low[(k + 1) * rows_each : (k + 2) * rows_each]
        spot = jnp.bitwise_xor(jnp.int32(plan.place(first + k)), jnp.bitwise_and(mine, PIECES // 2 - 1))
        kept_ref[spot, row : row + rows_each, :] = jnp.where(core, even, odd)
        sent_ref[spot, row : row + rows_each, :] = jnp.where(core, odd, even)


def halves(rows):
    return [shape((PIECES // 2, rows, D), bf16)] * 2


def call(kernel, outs, ins, specs, scratch=(), name=None):
    return pl.pallas_call(
        kernel,
        out_shape=list(outs),
        in_specs=specs,
        out_specs=[vmem()] * len(outs),
        scratch_shapes=list(scratch),
        compiler_params=pltpu.CompilerParams(vmem_limit_bytes=VMEM_LIMIT),
        name=name,
    )(*ins)


def ffn_ahead(values, gain, win, wout, entry_ref, hidden_ref, slope_ref):
    normed, _ = stats(values)
    entry = (normed * gain).astype(bf16)
    entry_ref[...] = entry
    total = jnp.zeros(values.shape, f32)
    for b in range(FF // D):
        cols = slice(b * D, (b + 1) * D)
        before = dot(entry, win[:, cols])
        sig = logistic(before)
        hidden = (before * sig).astype(bf16)
        hidden_ref[:, cols] = hidden
        slope_ref[:, cols] = slope_of(before, sig).astype(bf16)
        total = total + dot(hidden, wout[cols, :])
    return total


def ffn_behind(grad, values, gain, win, wout, entry_ref, hidden_ref, slope_ref, out_refs, plan, place_ref):
    normed, scale = stats(values)
    entry = entry_ref[...]
    branch = (0.5 * grad).astype(bf16)
    grad_entry = jnp.zeros(values.shape, f32)
    for b in range(FF // D):
        cols = slice(b * D, (b + 1) * D)
        put(out_refs, plan, place_ref, dot_rows(hidden_ref[:, cols], branch), 64, 64, 8 * b)
        grad_before = (dot_cols(branch, wout[cols, :]) * slope_ref[:, cols].astype(f32)).astype(bf16)
        put(out_refs, plan, place_ref, dot_rows(entry, grad_before), 16 * b, 16, 0)
        grad_entry = grad_entry + dot_cols(grad_before, win[:, cols])
    back, grad_gain = norm_back(grad_entry, normed, scale, gain)
    return grad + back, grad_gain


def ffn_first_up(frames, vec, win_parts, place):
    rows = frames.shape[0]
    n = len(win_parts)

    def kernel(place_ref, x_ref, vec_ref, *rest):
        wins = rest[:n]
        entry_ref, hidden_ref, slope_ref, win = rest[n:]
        normed, _ = stats(x_ref[...].astype(f32))
        entry = (normed * vec_ref[31:32, :]).astype(bf16)
        entry_ref[...] = entry
        join(place_ref, wins, win)
        for b in range(FF // D):
            cols = slice(b * D, (b + 1) * D)
            before = dot(entry, win[:, cols])
            sig = logistic(before)
            hidden_ref[:, cols] = (before * sig).astype(bf16)
            slope_ref[:, cols] = slope_of(before, sig).astype(bf16)

    return call(
        kernel,
        [shape((rows, D), bf16), shape((rows, FF), bf16), shape((rows, FF), bf16)],
        [place, frames, vec, *win_parts],
        [smem()] + [vmem()] * 2 + [vmem()] * n,
        [pltpu.VMEM((D, FF), bf16)],
        "ffn_first_up",
    )


def ffn_first_down(frames, hidden, wout_parts, place):
    rows = frames.shape[0]
    n = len(wout_parts)

    def kernel(place_ref, x_ref, hidden_ref, *rest):
        wouts = rest[:n]
        out_ref, wout = rest[n:]
        join(place_ref, wouts, wout)
        out_ref[...] = x_ref[...].astype(f32) + 0.5 * dot(hidden_ref[...], wout[...])

    return call(
        kernel,
        [shape((rows, D), f32)],
        [place, frames, hidden, *wout_parts],
        [smem()] + [vmem()] * 2 + [vmem()] * n,
        [pltpu.VMEM((FF, D), bf16)],
        "ffn_first_down",
    )[0]


def ffn_last(values, vec, cotangent, lengths, win_parts, wout_parts, place, plan):
    rows = values.shape[0]
    count = lengths.shape[0]
    n = len(win_parts)

    def kernel(place_ref, len_ref, x_ref, vec_ref, cot_ref, *rest):
        wins, wouts = rest[:n], rest[n : 2 * n]
        y_ref, dx_ref, gain_ref, *g_refs = rest[2 * n : 2 * n + 5]
        win, wout, entry_ref, hidden_ref, slope_ref = rest[2 * n + 5 :]
        join(place_ref, wins, win)
        join(place_ref, wouts, wout)
        x = x_ref[...]
        gain = vec_ref[35:36, :]
        total = ffn_ahead(x, gain, win, wout, entry_ref, hidden_ref, slope_ref)
        normed, scale = stats(x + 0.5 * total)
        top = vec_ref[36:37, :]
        y_ref[...] = (normed * top).astype(bf16)
        each = rows // count
        grads = []
        for s in range(count):
            spot = lax.broadcasted_iota(jnp.int32, (each, 1), 0)
            part = cot_ref[s * each : (s + 1) * each, :].astype(f32)
            grads.append(jnp.where(spot < len_ref[s], part, 0.0))
        back, grad_top = norm_back(jnp.concatenate(grads, axis=0), normed, scale, top)
        grad, grad_gain = ffn_behind(
            back, x, gain, win, wout, entry_ref, hidden_ref, slope_ref, g_refs, plan, place_ref
        )
        dx_ref[...] = grad
        gain_ref[...] = jnp.concatenate([grad_gain, grad_top, jnp.zeros((6, D), f32)], axis=0)

    return call(
        kernel,
        [shape((rows, D), bf16), shape((rows, D), f32), shape((8, D), f32), *halves(FFN_ROWS)],
        [place, lengths, values, vec, cotangent, *win_parts, *wout_parts],
        [smem(), smem()] + [vmem()] * 3 + [vmem()] * (2 * n),
        [
            pltpu.VMEM((D, FF), bf16),
            pltpu.VMEM((FF, D), bf16),
            pltpu.VMEM((rows, D), bf16),
            pltpu.VMEM((rows, FF), bf16),
            pltpu.VMEM((rows, FF), bf16),
        ],
        "ffn_last",
    )


def ffn_first_out(grad, hidden, slope, wout_parts, place, plan):
    rows = grad.shape[0]
    n = len(wout_parts)

    def kernel(place_ref, grad_ref, hidden_ref, slope_ref, *rest):
        wouts = rest[:n]
        before_ref, *g_refs = rest[n : n + 3]
        (wout,) = rest[n + 3 :]
        join(place_ref, wouts, wout)
        branch = (0.5 * grad_ref[...]).astype(bf16)
        for b in range(FF // D):
            cols = slice(b * D, (b + 1) * D)
            put(g_refs, plan, place_ref, dot_rows(hidden_ref[:, cols], branch), 0, 64, 8 * b)
            spread = dot_cols(branch, wout[cols, :])
            before_ref[:, cols] = (spread * slope_ref[:, cols].astype(f32)).astype(bf16)

    return call(
        kernel,
        [shape((rows, FF), bf16), *halves(64)],
        [place, grad, hidden, slope, *wout_parts],
        [smem()] + [vmem()] * 3 + [vmem()] * n,
        [pltpu.VMEM((FF, D), bf16)],
        "ffn_first_out",
    )


def ffn_first_in(grad, frames, vec, entry, before, win_parts, place, plan):
    rows = frames.shape[0]
    n = len(win_parts)

    def kernel(place_ref, grad_ref, x_ref, vec_ref, entry_ref, before_ref, *rest):
        wins = rest[:n]
        dx_ref, gain_ref, *g_refs = rest[n : n + 4]
        (win,) = rest[n + 4 :]
        join(place_ref, wins, win)
        low = entry_ref[...]
        grad_entry = jnp.zeros((rows, D), f32)
        for b in range(FF // D):
            cols = slice(b * D, (b + 1) * D)
            put(g_refs, plan, place_ref, dot_rows(low, before_ref[:, cols]), 16 * b, 16, 0)
            grad_entry = grad_entry + dot_cols(before_ref[:, cols], win[:, cols])
        normed, scale = stats(x_ref[...].astype(f32))
        back, grad_gain = norm_back(grad_entry, normed, scale, vec_ref[31:32, :])
        dx_ref[...] = (grad_ref[...] + back).astype(bf16)
        gain_ref[...] = jnp.concatenate([grad_gain, jnp.zeros((7, D), f32)], axis=0)

    return call(
        kernel,
        [shape((rows, D), bf16), shape((8, D), f32), *halves(64)],
        [place, grad, frames, vec, entry, before, *win_parts],
        [smem()] + [vmem()] * 5 + [vmem()] * n,
        [pltpu.VMEM((D, FF), bf16)],
        "ffn_first_in",
    )


def attend(values, vec, rel_table, lengths, parts, place, plan):
    rows = values.shape[0]
    count = lengths.shape[0]
    each = rows // count
    n = len(parts)
    pairs = HEADS // 2

    def kernel(place_ref, len_ref, x_ref, vec_ref, rel_ref, *rest):
        ws = rest[:n]
        out_ref, entry_ref, qkv_ref, prob_ref, mix_ref, weight, mixed = rest[n:]
        join(place_ref, ws, weight)
        x = x_ref[...]
        normed, _ = stats(x)
        entry = (normed * vec_ref[32:33, :]).astype(bf16)
        entry_ref[...] = entry
        for k in range(3):
            heads = dot(entry, weight[k]).astype(bf16)
            for p in range(pairs):
                qkv_ref[k, p] = heads[:, p * 128 : (p + 1) * 128]
        lane = lax.broadcasted_iota(jnp.int32, (1, 128), 1)
        table = rel_ref[...]
        spot = lax.broadcasted_iota(jnp.int32, (1, each), 1)

        def step(i, carry):
            s = i // pairs
            p = i % pairs
            span = pl.ds(pl.multiple_of(s * each, each), each)
            query = qkv_ref[0, p, span, :]
            keys = qkv_ref[1, p, span, :]
            vals = qkv_ref[2, p, span, :]
            valid = spot < len_ref[s]
            both = []
            for h in range(2):
                mask = (lane < HEAD) if h == 0 else (lane >= HEAD)
                mine = jnp.where(mask, query, jnp.zeros_like(query))
                raw = dot_cols(mine, keys)
                skew = pltpu.roll(dot_cols(mine, table), 0, 1, stride=1, stride_axis=0)[:, :each]
                scores = jnp.where(valid, (raw + skew) * 0.125, MASKED_SCORE)
                grown = jnp.exp(scores - jnp.max(scores, axis=-1, keepdims=True))
                low = (grown * (1.0 / jnp.sum(grown, axis=-1, keepdims=True))).astype(bf16)
                prob_ref[2 * i + h] = low
                both.append(dot(low, vals))
            mixed[p, span, :] = jnp.where(lane < HEAD, both[0], both[1]).astype(bf16)
            return carry

        lax.fori_loop(0, count * pairs, step, 0)
        mix = jnp.concatenate([mixed[p] for p in range(pairs)], axis=1)
        mix_ref[...] = mix
        out_ref[...] = x + dot(mix, weight[3])

    return call(
        kernel,
        [
            shape((rows, D), f32),
            shape((rows, D), bf16),
            shape((3, pairs, rows, 128), bf16),
            shape((count * HEADS, each, each), bf16),
            shape((rows, D), bf16),
        ],
        [place, lengths, values, vec, rel_table, *parts],
        [smem(), smem()] + [vmem()] * (3 + n),
        [pltpu.VMEM((4, D, D), bf16), pltpu.VMEM((pairs, rows, 128), bf16)],
        "attend",
    )


def attend_back(grad, values, vec, kept, rel_table, parts, place, plan, count):
    rows = values.shape[0]
    each = rows // count
    n = len(parts)
    pairs = HEADS // 2
    entry, qkv, prob, mix = kept
    width = rel_table.shape[0]

    def kernel(place_ref, grad_ref, x_ref, vec_ref, entry_ref, qkv_ref, prob_ref, mix_ref, rel_ref, *rest):
        ws = rest[:n]
        dx_ref, gain_ref, rel_out, *g_refs = rest[n : n + 5]
        weight, dmix, dqkv = rest[n + 5 :]
        join(place_ref, ws, weight)
        down = grad_ref[...]
        low = down.astype(bf16)
        put(g_refs, plan, place_ref, dot_rows(mix_ref[...], low), 48, 16, 0)
        spread = dot_cols(low, weight[3]).astype(bf16)
        for p in range(pairs):
            dmix[p] = spread[:, p * 128 : (p + 1) * 128]
        lane = lax.broadcasted_iota(jnp.int32, (1, 128), 1)
        table = rel_ref[...]
        flip = (
            lax.broadcasted_iota(jnp.int32, (each, each), 0)
            + lax.broadcasted_iota(jnp.int32, (each, each), 1)
            == each - 1
        ).astype(bf16)
        rel_out[...] = jnp.zeros_like(rel_out)

        def step(i, carry):
            s = i // pairs
            p = i % pairs
            span = pl.ds(pl.multiple_of(s * each, each), each)
            query = qkv_ref[0, p, span, :]
            keys = qkv_ref[1, p, span, :]
            vals = qkv_ref[2, p, span, :]
            outer = dmix[p, span, :]
            grad_q = jnp.zeros((each, 128), f32)
            grad_k = jnp.zeros((each, 128), f32)
            grad_v = jnp.zeros((each, 128), f32)
            grad_r = jnp.zeros((width, 128), f32)
            for h in range(2):
                mask = (lane < HEAD) if h == 0 else (lane >= HEAD)

                def pick(v):
                    return jnp.where(mask, v, jnp.zeros_like(v))

                dout = pick(outer)
                q_own = pick(query)
                prob_low = prob_ref[2 * i + h]
                prob_wide = prob_low.astype(f32)
                dprob = dot_cols(dout, vals)
                inner = jnp.sum(prob_wide * dprob, axis=-1, keepdims=True)
                dscore = (prob_wide * (dprob - inner)).astype(bf16)
                grad_v = grad_v + dot_rows(prob_low, dout)
                grad_k = grad_k + dot_rows(dscore, q_own)
                turned = dot(flip, dscore)
                wide = jnp.concatenate([turned, jnp.zeros((each, width - each), f32)], axis=1)
                skew = pltpu.roll(wide, width - each + 1, 1, stride=1, stride_axis=0).astype(bf16)
                along = dot(flip, skew).astype(bf16)
                grad_q = grad_q + dot(dscore, pick(keys)) + dot(along, pick(table))
                grad_r = grad_r + dot_rows(along, q_own)
            dqkv[0, p, span, :] = (grad_q * 0.125).astype(bf16)
            dqkv[1, p, span, :] = (grad_k * 0.125).astype(bf16)
            dqkv[2, p, span, :] = grad_v.astype(bf16)
            rel_out[...] += grad_r * 0.125
            return carry

        lax.fori_loop(0, count * pairs, step, 0)
        entry_low = entry_ref[...]
        grad_entry = jnp.zeros((rows, D), f32)
        for k in range(3):
            heads = jnp.concatenate([dqkv[k, p] for p in range(pairs)], axis=1)
            put(g_refs, plan, place_ref, dot_rows(entry_low, heads), 16 * k, 16, 0)
            grad_entry = grad_entry + dot_cols(heads, weight[k])
        normed, scale = stats(x_ref[...])
        back, grad_gain = norm_back(grad_entry, normed, scale, vec_ref[32:33, :])
        dx_ref[...] = down + back
        gain_ref[...] = jnp.concatenate([grad_gain, jnp.zeros((7, D), f32)], axis=0)

    return call(
        kernel,
        [
            shape((rows, D), f32),
            shape((8, D), f32),
            shape((width, 128), f32),
            *halves(ATTN_ROWS),
        ],
        [place, grad, values, vec, entry, qkv, prob, mix, rel_table, *parts],
        [smem()] + [vmem()] * (8 + n),
        [
            pltpu.VMEM((4, D, D), bf16),
            pltpu.VMEM((pairs, rows, 128), bf16),
            pltpu.VMEM((3, pairs, rows, 128), bf16),
        ],
        "attend_back",
    )


def convolve(values, vec, parts, place, plan, count):
    rows = values.shape[0]
    each = rows // count
    n = len(parts)
    cols = D // 128
    chunk = 64

    def kernel(place_ref, x_ref, vec_ref, *rest):
        ws = rest[:n]
        out_ref, entry_ref, gated_ref, sig_ref, conv_ref, act_ref, weight = rest[n:]
        join(place_ref, ws, weight)
        x = x_ref[...]
        normed, _ = stats(x)
        entry = (normed * vec_ref[33:34, :]).astype(bf16)
        entry_ref[...] = entry
        linear = dot(entry, weight[:, :D])
        sig = logistic(dot(entry, weight[:, D : 2 * D]))
        sig_ref[...] = sig
        gated = linear * sig
        for s in range(count):
            for c in range(cols):
                gated_ref[s, c, :LEAD, :] = jnp.zeros((LEAD, 128), f32)
                gated_ref[s, c, LEAD:, :] = gated[s * each : (s + 1) * each, c * 128 : (c + 1) * 128]
        for c in range(cols):
            taps = vec_ref[0:32, c * 128 : (c + 1) * 128]

            def step(i, carry):
                s = i // (each // chunk)
                t = (i % (each // chunk)) * chunk
                total = jnp.zeros((chunk, 128), f32)
                for k in range(KERNEL):
                    total = total + taps[k : k + 1] * gated_ref[s, c, pl.ds(t + k + LEAD - KERNEL + 1, chunk), :]
                conv_ref[pl.ds(pl.multiple_of(i * chunk, chunk), chunk), c * 128 : (c + 1) * 128] = total
                return carry

            lax.fori_loop(0, rows // chunk, step, 0)
        inner, _ = stats(conv_ref[...])
        act = inner * vec_ref[34:35, :]
        low = (act * logistic(act)).astype(bf16)
        act_ref[...] = low
        out_ref[...] = x + dot(low, weight[:, 2 * D :])

    return call(
        kernel,
        [
            shape((rows, D), f32),
            shape((rows, D), bf16),
            shape((count, cols, each + LEAD, 128), f32),
            shape((rows, D), f32),
            shape((rows, D), f32),
            shape((rows, D), bf16),
        ],
        [place, values, vec, *parts],
        [smem()] + [vmem()] * (2 + n),
        [pltpu.VMEM((D, 3 * D), bf16)],
        "convolve",
    )


def convolve_back(grad, values, vec, kept, parts, place, plan, count):
    rows = values.shape[0]
    each = rows // count
    n = len(parts)
    cols = D // 128
    entry, gated, sig, conved, act = kept

    def kernel(place_ref, grad_ref, x_ref, vec_ref, entry_ref, gated_ref, sig_ref, conv_ref, act_ref, *rest):
        ws = rest[:n]
        dx_ref, gain_ref, taps_out, *g_refs = rest[n : n + 5]
        weight, dconv, dgated = rest[n + 5 :]
        join(place_ref, ws, weight)
        down = grad_ref[...]
        low = down.astype(bf16)
        put(g_refs, plan, place_ref, dot_rows(act_ref[...], low), 32, 16, 0)
        inner, inner_scale = stats(conv_ref[...])
        inner_gain = vec_ref[34:35, :]
        act_in = inner * inner_gain
        grad_act = dot_cols(low, weight[:, 2 * D :]) * slope_of(act_in, logistic(act_in))
        grad_conv, gain_inner = norm_back(grad_act, inner, inner_scale, inner_gain)
        for s in range(count):
            for c in range(cols):
                dconv[s, c, :each, :] = grad_conv[s * each : (s + 1) * each, c * 128 : (c + 1) * 128]
                dconv[s, c, each:, :] = jnp.zeros((LEAD, 128), f32)
        for c in range(cols):
            lanes = slice(c * 128, (c + 1) * 128)
            taps = vec_ref[0:32, lanes]

            def step(i, sums):
                s = i // (each // 8)
                t = (i % (each // 8)) * 8
                here = dconv[s, c, pl.ds(pl.multiple_of(t, 8), 8), :]
                total = jnp.zeros((8, 128), f32)
                new = []
                for k in range(KERNEL):
                    new.append(sums[k] + here * gated_ref[s, c, pl.ds(t + k + LEAD - KERNEL + 1, 8), :])
                    total = total + taps[k : k + 1] * dconv[s, c, pl.ds(t + KERNEL - 1 - k, 8), :]
                dgated[pl.ds(pl.multiple_of(i * 8, 8), 8), lanes] = total
                return tuple(new)

            sums = lax.fori_loop(0, rows // 8, step, tuple(jnp.zeros((8, 128), f32) for _ in range(KERNEL)))
            found = [jnp.sum(v, axis=0, keepdims=True) for v in sums]
            taps_out[:, lanes] = jnp.concatenate(found + [jnp.zeros((1, 128), f32)], axis=0)
        grad_gated = dgated[...]
        sig_wide = sig_ref[...]
        linear_sig = jnp.concatenate(
            [
                jnp.concatenate([gated_ref[s, c, LEAD:, :] for c in range(cols)], axis=1)
                for s in range(count)
            ],
            axis=0,
        )
        grad_one = (grad_gated * sig_wide).astype(bf16)
        grad_two = (grad_gated * linear_sig * (1.0 - sig_wide)).astype(bf16)
        entry_low = entry_ref[...]
        put(g_refs, plan, place_ref, dot_rows(entry_low, grad_one), 0, 16, 0)
        put(g_refs, plan, place_ref, dot_rows(entry_low, grad_two), 16, 16, 0)
        grad_entry = dot_cols(grad_one, weight[:, :D]) + dot_cols(grad_two, weight[:, D : 2 * D])
        normed, scale = stats(x_ref[...])
        back, gain_outer = norm_back(grad_entry, normed, scale, vec_ref[33:34, :])
        dx_ref[...] = down + back
        gain_ref[...] = jnp.concatenate([gain_outer, gain_inner, jnp.zeros((6, D), f32)], axis=0)

    return call(
        kernel,
        [
            shape((rows, D), f32),
            shape((8, D), f32),
            shape((32, D), f32),
            *halves(CONV_ROWS),
        ],
        [place, grad, values, vec, entry, gated, sig, conved, act, *parts],
        [smem()] + [vmem()] * (8 + n),
        [
            pltpu.VMEM((D, 3 * D), bf16),
            pltpu.VMEM((count, cols, each + LEAD, 128), f32),
            pltpu.VMEM((rows, D), f32),
        ],
        "convolve_back",
    )


def adam(weight, moment, square, grad):
    new_moment = BETA_FIRST * moment + (1.0 - BETA_FIRST) * grad
    new_square = BETA_SECOND * square + (1.0 - BETA_SECOND) * grad * grad
    first = new_moment * (1.0 / (1.0 - BETA_FIRST**STEP))
    second = new_square * (1.0 / (1.0 - BETA_SECOND**STEP))
    update = first / (jnp.sqrt(second) + ADAM_EPSILON) + WEIGHT_DECAY * weight
    return new_moment, new_square, update


def folded(values):
    squares = jnp.sum((values * values).reshape(-1, values.shape[-1]), axis=0, keepdims=True)
    total = squares[:, :128]
    for c in range(1, values.shape[-1] // 128):
        total = total + squares[:, c * 128 : (c + 1) * 128]
    return total


def update_matrix(layer, pieces, block, spots, states, given, name):
    count = spots.shape[0]
    rows, cols = states[0].shape[1] // count, states[0].shape[2]
    given = given or ()

    half = count // 2

    def kernel(spot_ref, g0_near, g0_far, g1_near, g1_far, w_ref, m_ref, q_ref, *rest):
        g_out, u_out, m_out, q_out, sums = rest[len(given) :]
        index = 2 * pl.program_id(0)

        @pl.when(pl.program_id(0) == 0)
        def _():
            sums[...] = jnp.zeros_like(sums)

        grads = []
        for k, near, far in ((0, g0_near, g0_far), (1, g1_near, g1_far)):
            raw = jnp.where(spot_ref[index + k] < half, near[0], far[0]).astype(f32)
            grads.append(jnp.concatenate([raw[k * rows : (k + 1) * rows] for k in range(cols // D)], axis=1))
        grad = jnp.concatenate(grads, axis=0)
        weight = w_ref[0]
        new_moment, new_square, update = adam(weight, m_ref[0], q_ref[0], grad)
        g_out[0] = grad
        u_out[0] = update
        m_out[0] = new_moment
        q_out[0] = new_square
        sums[...] += jnp.concatenate([folded(weight), folded(update), jnp.zeros((6, 128), f32)], axis=0)

    tile = pl.BlockSpec((1, 2 * rows, cols), lambda p, spot: (layer, p, 0))
    return pl.pallas_call(
        kernel,
        out_shape=[shape(states[0].shape, f32)] * 4 + [shape((8, 128), f32)],
        grid_spec=pltpu.PrefetchScalarGridSpec(
            num_scalar_prefetch=1,
            grid=(count // 2,),
            in_specs=[
                pl.BlockSpec((1, 64, D), lambda p, spot, k=k: (spot[2 * p + k] % half, block, 0))
                for k in (0, 0, 1, 1)
            ]
            + [tile] * 3
            + [pl.BlockSpec(memory_space=pl.ANY)] * len(given),
            out_specs=[tile] * 4 + [pl.BlockSpec((8, 128), lambda p, spot: (0, 0))],
        ),
        input_output_aliases={8 + k: k for k in range(len(given))},
        compiler_params=pltpu.CompilerParams(vmem_limit_bytes=STREAM_LIMIT),
        name=name,
    )(spots, *pieces, *pieces, *states, *given)


def move_layer(layer, win, in_update, in_factor, wout, out_update, out_factor):
    steps = 4
    tiles = [pl.BlockSpec((1, w.shape[1] // steps, w.shape[2]), lambda p: (layer, p, 0)) for w in (win, wout)]

    def kernel(factor_ref, w0, u0, w1, u1, out0, out1):
        out0[...] = w0[...] - (LEARN_RATE * factor_ref[0]) * u0[...]
        out1[...] = w1[...] - (LEARN_RATE * factor_ref[1]) * u1[...]

    return pl.pallas_call(
        kernel,
        out_shape=[shape(win.shape, f32), shape(wout.shape, f32)],
        grid=(steps,),
        in_specs=[smem(), tiles[0], tiles[0], tiles[1], tiles[1]],
        out_specs=tiles,
        input_output_aliases={2: 0, 4: 1},
        compiler_params=pltpu.CompilerParams(vmem_limit_bytes=STREAM_LIMIT),
        name="move_layer",
    )(jnp.stack([in_factor, out_factor]), win, in_update, wout, out_update)


def move_rest(attn, attn_update, conv, conv_update, factors):
    steps = 4
    rows = attn.shape[1] // steps
    attn_tile = pl.BlockSpec((4, rows, D), lambda p: (0, p, 0))
    conv_tile = pl.BlockSpec((rows, 3 * D), lambda p: (p, 0))

    def kernel(factor_ref, w0, u0, w1, u1, out0, out1):
        for k in range(4):
            out0[k] = w0[k] - (LEARN_RATE * factor_ref[k]) * u0[k]
        for k, lanes in ((4, slice(0, 2 * D)), (5, slice(2 * D, 3 * D))):
            out1[:, lanes] = w1[:, lanes] - (LEARN_RATE * factor_ref[k]) * u1[:, lanes]

    return pl.pallas_call(
        kernel,
        out_shape=[shape(attn.shape, f32), shape(conv.shape, f32)],
        grid=(steps,),
        in_specs=[smem(), attn_tile, attn_tile, conv_tile, conv_tile],
        out_specs=[attn_tile, conv_tile],
        input_output_aliases={2: 0, 4: 1},
        compiler_params=pltpu.CompilerParams(vmem_limit_bytes=STREAM_LIMIT),
        name="move_rest",
    )(factors, attn, attn_update, conv, conv_update)


def packed(gains_first, gains_attn, gains_conv, gains_last, taps, rel_wide, each):
    edge = 2 * each - BACK

    def kernel(g0, g1, g2, g4, taps_ref, rel_ref, out_ref, rel):
        out_ref[...] = jnp.zeros_like(out_ref)
        out_ref[0:KERNEL, :] = taps_ref[0:KERNEL, :]
        out_ref[31:32, :] = g0[0:1, :]
        out_ref[32:33, :] = g1[0:1, :]
        out_ref[33:35, :] = g2[0:2, :]
        out_ref[35:37, :] = g4[0:2, :]
        half = rel_ref[:, :HEAD] + rel_ref[:, HEAD:]
        rel[...] = jnp.zeros_like(rel)
        rel[0:1, :] = jnp.sum(half[each : edge + 8] * (lax.broadcasted_iota(jnp.int32, (each - BACK + 8, 1), 0) <= each - BACK), axis=0, keepdims=True)
        rel[0:BACK, :] = rel[0:BACK, :] + half[edge:] * (lax.broadcasted_iota(jnp.int32, (BACK, 1), 0) > 0)
        rel[BACK : BACK + AHEAD, :] = half[:AHEAD]
        rel[RELS - 1 : RELS, :] = jnp.sum(half[AHEAD:each], axis=0, keepdims=True)
        for b in range(5):
            out_ref[40:56, b * HEAD : (b + 1) * HEAD] = rel[b * 16 : b * 16 + 16, :]

    return call(
        kernel,
        [shape((56, D), f32)],
        [gains_first, gains_attn, gains_conv, gains_last, taps, rel_wide],
        [vmem()] * 6,
        [pltpu.VMEM((80, HEAD), f32)],
        "packed",
    )[0]


def update_rest(pieces, spots, attn, conv):
    count = spots.shape[0]
    rows = 2 * (attn[0].shape[1] // count)

    half = count // 2

    def kernel(spot_ref, g0_near, g0_far, g1_near, g1_far, wa, ma, qa, wc, mc, qc, *outs):
        ga_out, ua_out, ma_out, qa_out, qo_out, gc_out, uc_out, mc_out, qc_out, sums = outs
        index = pl.program_id(0)

        @pl.when(index == 0)
        def _():
            sums[...] = jnp.zeros_like(sums)

        raws = [
            jnp.where(spot_ref[2 * index + k] < half, near[0], far[0])
            for k, near, far in ((0, g0_near, g0_far), (1, g1_near, g1_far))
        ]
        found = []
        for k in range(4):
            low = CONV_ROWS + k * 16
            grad = jnp.concatenate([g[low : low + 16] for g in raws], axis=0).astype(f32)
            weight = wa[k]
            new_moment, new_square, update = adam(weight, ma[k], qa[k], grad)
            ga_out[k] = grad
            ua_out[k] = update
            ma_out[k] = new_moment
            if k < 3:
                qa_out[k] = new_square
            else:
                qo_out[...] = new_square
            found += [folded(weight), folded(update)]
        for low, high in ((0, 2), (2, 3)):
            lanes = slice(low * D, high * D)
            parts = [
                jnp.concatenate([g[k * 16 : (k + 1) * 16] for k in range(low, high)], axis=1) for g in raws
            ]
            grad = jnp.concatenate(parts, axis=0).astype(f32)
            weight = wc[:, lanes]
            new_moment, new_square, update = adam(weight, mc[:, lanes], qc[:, lanes], grad)
            gc_out[:, lanes] = grad
            uc_out[:, lanes] = update
            mc_out[:, lanes] = new_moment
            qc_out[:, lanes] = new_square
            found += [folded(weight), folded(update)]
        sums[...] += jnp.concatenate(found + [jnp.zeros((4, 128), f32)], axis=0)

    attn_block = pl.BlockSpec((4, rows, D), lambda p, spot: (0, p, 0))
    conv_block = pl.BlockSpec((rows, 3 * D), lambda p, spot: (p, 0))
    three = pl.BlockSpec((3, rows, D), lambda p, spot: (0, p, 0))
    one = pl.BlockSpec((rows, D), lambda p, spot: (p, 0))
    side = attn[0].shape[1]
    return pl.pallas_call(
        kernel,
        out_shape=[shape(attn[0].shape, f32)] * 3
        + [shape((3, side, D), f32), shape((side, D), f32)]
        + [shape(conv[0].shape, f32)] * 4
        + [shape((16, 128), f32)],
        grid_spec=pltpu.PrefetchScalarGridSpec(
            num_scalar_prefetch=1,
            grid=(count // 2,),
            in_specs=[
                pl.BlockSpec((1, CONV_ROWS + ATTN_ROWS, D), lambda p, spot, k=k: (spot[2 * p + k] % half, 0, 0))
                for k in (0, 0, 1, 1)
            ]
            + [attn_block] * 3
            + [conv_block] * 3,
            out_specs=[attn_block] * 3
            + [three, one]
            + [conv_block] * 4
            + [pl.BlockSpec((16, 128), lambda p, spot: (0, 0))],
        ),
        compiler_params=pltpu.CompilerParams(vmem_limit_bytes=STREAM_LIMIT),
        name="update_rest",
    )(spots, *pieces, *pieces, *attn, *conv)


def move(weight, update, factor):
    return weight - LEARN_RATE * factor * update


def ratio_of(sums):
    weight, update = sums[0::2], sums[1::2]
    return jnp.sqrt(weight), jnp.sqrt(update), jnp.sqrt(weight) / jnp.sqrt(update + RATIO_EPSILON)


def body(
    frames,
    lengths,
    cotangent,
    ffn_in,
    ffn_in_moment,
    ffn_in_square,
    ffn_out,
    ffn_out_moment,
    ffn_out_square,
    attn_proj,
    attn_moment,
    attn_square,
    conv_proj,
    conv_moment,
    conv_square,
    vectors,
    vectors_moment,
    vectors_square,
    rel_keys,
    rel_moment,
    rel_square,
):
    groups, shards = lax.axis_size("group"), lax.axis_size("shard")
    plan = Plan(groups, shards)
    group, shard = lax.axis_index("group"), lax.axis_index("shard")
    core = jnp.bitwise_and(group, 1)
    count, each, _ = frames.shape
    mine = jnp.int32(0)
    for step in plan.order:
        bit = jnp.right_shift(group if step[0] == "group" else shard, step[1]) & 1
        mine = mine * 2 + bit
    kept = jnp.int32(0)
    for step in plan.kept:
        kept = kept * 2 + (jnp.right_shift(group, step[1]) & 1)
    spots = jnp.array([plan.kept_place(p) for p in range(plan.owned)], jnp.int32) ^ kept
    place = jnp.stack([shard, core, mine]).astype(jnp.int32)

    first_halves = rounded_halves(plan, core, (ffn_in, 1, 0), (ffn_out, 1, 0))
    rows, halves_left = rounded_rows(plan, core, ffn_in, ffn_out, attn_proj, conv_proj)
    win0, wout0 = (Fetch(w, 0, plan, r, v, 0) for w, r, v in zip((ffn_in, ffn_out), rows, first_halves))
    watt = Fetch(attn_proj, 1, plan, rows[4], halves_left[0])
    wconv = Fetch(conv_proj, 0, plan, rows[5], halves_left[1])
    win1, wout1 = (Fetch(w, 0, plan, r, v, 1) for w, r, v in zip((ffn_in, ffn_out), rows[2:4], halves_left[2:]))
    win0.near()
    vec = lax.all_gather(vectors.astype(bf16), "shard", axis=1, tiled=True) if shards != 2 else None
    if vec is None:
        (low,) = gate([vectors.astype(bf16)], [first_halves[0]])
        other = swap(low, ("shard", 0))
        vec = jnp.where(shard == 0, jnp.concatenate([low, other], 1), jnp.concatenate([other, low], 1))
    vec = jnp.concatenate([vec.astype(f32), jnp.zeros((3, D), f32)], axis=0)
    rel_low = rel_keys.astype(bf16)
    table = jnp.concatenate(
        [
            rel_low[BACK:],
            jnp.broadcast_to(rel_low[RELS - 1 :], (each - AHEAD - 1, HEAD)),
            jnp.broadcast_to(rel_low[:1], (each - BACK, HEAD)),
            rel_low[:BACK],
        ],
        axis=0,
    )
    table = jnp.concatenate([table, table], axis=1)

    flat = frames.reshape(count * each, D)
    if shards == 2:
        order((win0,), (rows[0],))
    order((wout0,), (win0.value, vec))
    wout0.near()
    win0 = win0.far()
    entry0, hidden0, slope0 = ffn_first_up(flat, vec, win0, place)
    order((watt,), (wout0.value, entry0))
    watt.near()
    order((wout0,), (entry0,))
    order((wconv,), (watt.value,))
    order((win1,), (watt.value,))
    wconv.near()
    win1.near()
    wout0 = wout0.far()
    hidden0, watt.value = gate([hidden0, watt.value], [entry0])
    watt = watt.far()
    x1 = ffn_first_down(flat, hidden0, wout0, place)
    x2, *kept_attn = attend(x1, vec, table, lengths, watt, place, plan)
    order((wconv,), (x2,))
    order((wout1,), (x2,))
    wout1.near()
    wconv = wconv.far()
    x3, *kept_conv = convolve(x2, vec, wconv, place, plan, count)
    order((win1,), (x3,))
    win1 = win1.far()
    order((wout1,), (x3,))
    wout1 = wout1.far()
    output, d3, gains_last, *pieces = ffn_last(
        x3, vec, cotangent.reshape(count * each, D), lengths, win1, wout1, place, plan
    )
    last = Chain(*pieces, plan)
    d2, gains_conv, taps, *pieces = beside(
        [last], lambda d: convolve_back(d, x2, vec, kept_conv, wconv, place, plan, count), [d3], 1
    )
    conv = Chain(*pieces, plan)
    d1, gains_attn, rel_wide, *pieces = beside(
        [last, conv], lambda d: attend_back(d, x1, vec, kept_attn, table, watt, place, plan, count), [d2], 1
    )
    attn = Chain(*pieces, plan)
    before0, *pieces = beside(
        [last, conv, attn], lambda d: ffn_first_out(d, hidden0, slope0, wout0, place, plan), [d1], 0
    )
    first_out = Chain(*pieces, plan)
    early = [last, attn, first_out] if len(conv.todo) < len(attn.todo) else [last, conv, attn, first_out]
    d0, gains_first, *pieces = beside(
        early, lambda b: ffn_first_in(d1, flat, vec, entry0, b, win0, place, plan), [before0], 1
    )
    first_in = Chain(*pieces, plan)
    middle = merged(conv, attn, plan)
    small = Everywhere(packed(gains_first, gains_attn, gains_conv, gains_last, taps, rel_wide, each), plan)
    advance([last, middle, first_out, first_in, small], 1)
    advance([last, middle, first_in, small], 1)
    first = merged(first_out, first_in, plan)
    chains = [last, middle, first, small]
    advance(chains, len(last.todo))
    in_states = (ffn_in, ffn_in_moment, ffn_in_square)
    out_states = (ffn_out, ffn_out_moment, ffn_out_square)
    *half_out, sums_out1 = beside(
        chains, lambda *v: update_matrix(1, v, 1, spots, out_states, None, "update_out1"), last.kept, -1
    )
    *half_in, sums_in1 = beside(
        chains, lambda *v: update_matrix(1, v, 0, spots, in_states, None, "update_in1"), last.kept, -1
    )
    advance(chains, len(middle.todo))
    attn_states = (attn_proj, attn_moment, attn_square)
    conv_states = (conv_proj, conv_moment, conv_square)
    (attn_grad, attn_up, attn_m, attn_q, attn_qo, conv_grad, conv_up, conv_m, conv_q, sums_rest) = beside(
        chains, lambda *v: update_rest(v, spots, attn_states, conv_states), middle.kept, -1
    )
    advance([small], len(small.todo))
    small = small.kept
    wide = vectors.shape[1]
    vec_grad = lax.dynamic_slice(small, (0, shard * wide), (KERNEL + 6, wide))
    rel_grad = jnp.concatenate([small[40:56, b * HEAD : (b + 1) * HEAD] for b in range(5)], axis=0)[:RELS]
    vec_m, vec_q, vec_up = adam(vectors, vectors_moment, vectors_square, vec_grad)
    rel_m, rel_q, rel_up = adam(rel_keys, rel_moment, rel_square, rel_grad)

    vec_sums = []
    for part in (vectors, vec_up):
        squares = jnp.sum(part * part, axis=1)
        vec_sums.append(jnp.concatenate([jnp.sum(squares[:KERNEL])[None], squares[KERNEL:]]))
    early = jnp.sum(jnp.concatenate([sums_in1[:2], sums_out1[:2], sums_rest[:12]], axis=0), axis=1)
    early = sum_shards(jnp.concatenate([early, jnp.stack(vec_sums, axis=1).reshape(-1)]), plan)
    early_ratio = ratio_of(early)
    fast = early_ratio[2]
    half_in[1], half_out[1] = beside(
        chains,
        lambda u: move_layer(1, ffn_in, u, fast[0], ffn_out, half_out[1], fast[1]),
        [half_in[1]],
        0,
    )
    advance(chains, len(first.todo))
    out_grad, out_up, out_m, out_q, sums_out0 = update_matrix(
        0, first.kept, 0, spots, out_states, half_out, "update_out0"
    )
    in_grad, in_up, in_m, in_q, sums_in0 = update_matrix(
        0, first.kept, 1, spots, in_states, half_in, "update_in0"
    )
    final = sum_shards(jnp.sum(jnp.concatenate([sums_in0[:2], sums_out0[:2]], axis=0), axis=1), plan)
    rel_sums = jnp.stack([jnp.sum(rel_keys * rel_keys), jnp.sum(rel_up * rel_up)])
    late_ratio = ratio_of(rel_sums)
    final_ratio = ratio_of(final)

    def spread(n):
        e, l = early_ratio[n], late_ratio[n]
        none = jnp.zeros((1,), f32)
        return jnp.concatenate([none, e[0:1], none, e[1:2], e[2:15], l[0:1]])

    column = lax.broadcasted_iota(jnp.int32, (2, 18), 1)
    last_in = jnp.stack([final_ratio[0][0], final_ratio[1][0]])[:, None]
    last_out = jnp.stack([final_ratio[0][1], final_ratio[1][1]])[:, None]
    known = jnp.stack([spread(0), spread(1)])
    trust_norms = jnp.where(column == 0, last_in, jnp.where(column == 2, last_out, known))
    ffn_in_new, ffn_out_new = move_layer(
        0, ffn_in, in_up, final_ratio[2][0], ffn_out, out_up, final_ratio[2][1]
    )
    attn_new, conv_new = move_rest(attn_proj, attn_up, conv_proj, conv_up, fast[2:8])
    vec_factor = jnp.concatenate([jnp.full((KERNEL,), fast[8]), fast[9:15]])[:, None]
    return (
        output.reshape(frames.shape),
        d0.reshape(frames.shape),
        in_grad,
        ffn_in_new,
        in_m,
        in_q,
        out_grad,
        ffn_out_new,
        out_m,
        out_q,
        attn_grad,
        attn_new,
        attn_m,
        attn_q,
        attn_qo,
        conv_grad,
        conv_new,
        conv_m,
        conv_q,
        vec_grad,
        move(vectors, vec_up, vec_factor),
        vec_m,
        vec_q,
        rel_grad,
        move(rel_keys, rel_up, late_ratio[2][0]),
        rel_m,
        rel_q,
        trust_norms,
    )


def solution(mesh):
    return jax.shard_map(
        body,
        mesh=mesh,
        in_specs=(
            P(("group", "shard"), None, None),
            P(("group", "shard")),
            P(("group", "shard"), None, None),
            P(None, "shard", None),
            P(None, "shard", None),
            P(None, "shard", None),
            P(None, "shard", None),
            P(None, "shard", None),
            P(None, "shard", None),
            P(None, "shard", None),
            P(None, "shard", None),
            P(None, "shard", None),
            P("shard", None),
            P("shard", None),
            P("shard", None),
            P(None, "shard"),
            P(None, "shard"),
            P(None, "shard"),
            P(),
            P(),
            P(),
        ),
        out_specs=(
            P(("group", "shard"), None, None),
            P(("group", "shard"), None, None),
            P(None, "shard", None),
            P(None, "shard", None),
            P(None, "shard", None),
            P(None, "shard", None),
            P(None, "shard", None),
            P(None, "shard", None),
            P(None, "shard", None),
            P(None, "shard", None),
            P(None, "shard", None),
            P(None, "shard", None),
            P(None, "shard", None),
            P(None, "shard", None),
            P("shard", None),
            P("shard", None),
            P("shard", None),
            P("shard", None),
            P("shard", None),
            P(None, "shard"),
            P(None, "shard"),
            P(None, "shard"),
            P(None, "shard"),
            P(),
            P(),
            P(),
            P(),
            P(),
        ),
        check_vma=False,
    )
```

profile of v0, /device:TPU:0, one launch (start us, length us, event | category | flops | bytes accessed | tf_op | source)
XLA Modules:
  0.0 354.5 jit_solution(10083350818402576204)
XLA Ops:
  0.7 2.7 rounded_halves.1
  3.4 3.0 collective-permute-start.1
  26.2 3.8 %ffn_first_up.1 = (bf16[512,512]{1,0:T(8,128)(2,1)S(1)}, bf16[512,2048]{1,0:T(8,128)(2,1)S(1)}, bf16[512,2048]{1,0:T(8,128)(2,1)S(1)}) custom-call(s32[3]{0:T(128)S(1)} %pad_add_fusion.place_ref, bf16[512,512]{1,0:T(8,128)(2,1)S(1)} %bitcast.30, f32[40,512]{1,0:T(8,128)S(1)} %pad_convert_fusion.vec_ref, bf16[256,2048]{1,0:T(8,128)(2,1)S(1)} %copy-done.6, ...), custom_call_target="tpu_custom_call" | custom-call | tf_op jit(solution)/shard_map/ffn_first_up/pallas_call | solution.py:351
  32.1 3.8 %collective-permute-done.3.rest_1_ = bf16[512,512]{1,0:T(8,128)(2,1)} collective-permute-done((bf16[512,512]{1,0:T(8,128)(2,1)}, bf16[512,512]{1,0:T(8,128)(2,1)}, u32[]{:S(2)}, u32[]{:S(2)}) %collective-permute-start.3) | collective-permute-done | bytes 524320 | tf_op jit(solution)/shard_map/ppermute | solution.py:119
  37.7 12.0 %collective-permute-done.4.rest_1_ = bf16[4,128,512]{2,1,0:T(8,128)(2,1)} collective-permute-done((bf16[4,128,512]{2,1,0:T(8,128)(2,1)S(1)}, bf16[4,128,512]{2,1,0:T(8,128)(2,1)}, u32[]{:S(2)}, u32[]{:S(2)}) %collective-permute-start.4) | collective-permute-done | bytes 524320 | tf_op jit(solution)/shard_map/ppermute | solution.py:119
  54.1 2.7 ffn_first_down.1.x_ref
  56.8 12.2 %attend.1 = (f32[512,512]{1,0:T(8,128)S(1)}, bf16[512,512]{1,0:T(8,128)(2,1)S(1)}, bf16[3,4,512,128]{3,2,1,0:T(8,128)(2,1)S(1)}, bf16[16,256,256]{2,1,0:T(8,128)(2,1)S(1)}, bf16[512,512]{1,0:T(8,128)(2,1)S(1)}) custom-call(s32[3]{0:T(128)S(1)} %pad_add_fusion.place_ref, s32[2]{0:T(128)S(1)} %copy-done.25, f32[512,512]{1,0:T(8,128)S(1)} %ffn_first_down.1.x_ref, ...), custom_call_target="tpu_custom_call" | custom-call | tf_op jit(solution)/shard_map/attend/pallas_call | solution.py:351
  72.4 5.7 %convolve.1 = (f32[512,512]{1,0:T(8,128)S(1)}, bf16[512,512]{1,0:T(8,128)(2,1)S(1)}, f32[2,4,288,128]{3,2,1,0:T(8,128)S(1)}, f32[512,512]{1,0:T(8,128)S(1)}, f32...) custom-call(s32[3]{0:T(128)S(1)} %pad_add_fusion.place_ref, f32[512,512]{1,0:T(8,128)S(1)} %get-tuple-element.187.x_ref, ...), custom_call_target="tpu_custom_call" | custom-call | tf_op jit(solution)/shard_map/convolve/pallas_call | solution.py:351
  78.3 6.5 %collective-permute-done.11.rest_4_ = bf16[512,512]{1,0:T(8,128)(2,1)S(1)} collective-permute-done((bf16[512,512]{1,0:T(8,128)(2,1)S(1)}, bf16[512,512]{1,0:T(8,128)(2,1)S(1)}, u32[]{:S(2)}, u32[]{:S(2)}) %collective-permute-start.11) | collective-permute-done | bytes 524320 | tf_op jit(solution)/shard_map/ppermute | solution.py:119
  86.7 10.4 %ffn_last.1 = (bf16[512,512]{1,0:T(8,128)(2,1)}, f32[512,512]{1,0:T(8,128)S(1)}, f32[8,512]{1,0:T(8,128)S(1)}, bf16[16,128,512]{2,1,0:T(8,128)(2,1)S(1)}, bf16[16,128,512]{2,1,0:T(8,128)(2,1)S(1)}) custom-call(s32[3]{0:T(128)S(1)} %pad_add_fusion.place_ref, s32[2]{0:T(128)S(1)} %copy-done.25, f32[512,512]{1,0:T(8,128)S(1)} %get-tuple-element.192.x_ref, ...), custom_call_target="tpu_custom_call" | custom-call | tf_op jit(solution)/shard_map/ffn_last/pallas_call | solution.py:351
  97.2 15.3 %convolve_back.1 = (f32[512,512]{1,0:T(8,128)S(1)}, f32[8,512]{1,0:T(8,128)S(1)}, f32[32,512]{1,0:T(8,128)S(1)}, bf16[16,48,512]{2,1,0:T(8,128)(2,1)S(1)}, bf16[16,48,512]{2,1,0:T(8,128)(2,1)S(1)}) custom-call(s32[3]{0:T(128)S(1)} %pad_add_fusion.place_ref, f32[512,512]{1,0:T(8,128)S(1)} %get-tuple-element.204.grad_ref, ...), custom_call_target="tpu_custom_call" | custom-call | tf_op jit(solution)/shard_map/convolve_back/pallas_call | solution.py:351
  115.3 28.2 %attend_back.1 = (f32[512,512]{1,0:T(8,128)S(1)}, f32[8,512]{1,0:T(8,128)S(1)}, f32[512,128]{1,0:T(8,128)S(1)}, bf16[16,64,512]{2,1,0:T(8,128)(2,1)S(1)}, bf16[16,64,512]{2,1,0:T(8,128)(2,1)S(1)}) custom-call(s32[3]{0:T(128)S(1)} %pad_add_fusion.place_ref, f32[512,512]{1,0:T(8,128)S(1)} %get-tuple-element.215.grad_ref, f32[512,512]{1,0:T(8,128)S(1)} %ffn_first_down.1.x_ref, ...), custom_call_target="tpu_custom_call" | custom-call | tf_op jit(solution)/shard_map/attend_back/pallas_call | solution.py:351
  146.5 3.7 %ffn_first_out.1 = (bf16[512,2048]{1,0:T(8,128)(2,1)S(1)}, bf16[16,64,512]{2,1,0:T(8,128)(2,1)S(1)}, bf16[16,64,512]{2,1,0:T(8,128)(2,1)S(1)}) custom-call(s32[3]{0:T(128)S(1)} %pad_add_fusion.place_ref, f32[512,512]{1,0:T(8,128)S(1)} %get-tuple-element.226.grad_ref, bf16[512,2048]{1,0:T(8,128)(2,1)S(1)} %get-tuple-element.182.hidden_ref, ...), custom_call_target="tpu_custom_call" | custom-call | tf_op jit(solution)/shard_map/ffn_first_out/pallas_call | solution.py:351
  152.1 3.9 %collective-permute-done.18 = bf16[8,48,512]{2,1,0:T(8,128)(2,1)S(1)} collective-permute-done((bf16[8,48,512]{2,1,0:T(8,128)(2,1)S(1)}, bf16[8,48,512]{2,1,0:T(8,128)(2,1)S(1)}, u32[]{:S(2)}, u32[]{:S(2)}) %collective-permute-start.18) | collective-permute-done | bytes 393248 | tf_op jit(solution)/shard_map/ppermute | solution.py:119
  156.1 2.8 collective-permute-done.16
  160.8 4.7 %ffn_first_in.1 = (bf16[512,512]{1,0:T(8,128)(2,1)}, f32[8,512]{1,0:T(8,128)S(1)}, bf16[16,64,512]{2,1,0:T(8,128)(2,1)S(1)}, bf16[16,64,512]{2,1,0:T(8,128)(2,1)S(1)}) custom-call(s32[3]{0:T(128)S(1)} %pad_add_fusion.place_ref, f32[512,512]{1,0:T(8,128)S(1)} %get-tuple-element.226.grad_ref, bf16[512,512]{1,0:T(8,128)(2,1)S(1)} %bitcast.32, ...), custom_call_target="tpu_custom_call" | custom-call | tf_op jit(solution)/shard_map/ffn_first_in/pallas_call | solution.py:351
  169.0 2.6 collective-permute-start.23
  173.0 5.3 %collective-permute-done.23 = bf16[1,128,512]{2,1,0:T(8,128)(2,1)S(1)} collective-permute-done((bf16[1,128,512]{2,1,0:T(8,128)(2,1)S(1)}, bf16[1,128,512]{2,1,0:T(8,128)(2,1)S(1)}, u32[]{:S(2)}, u32[]{:S(2)}) %collective-permute-start.23) | collective-permute-done | bytes 131104 | tf_op jit(solution)/shard_map/ppermute | solution.py:119
  184.5 2.6 collective-permute-start.27
  192.9 6.7 %collective-permute-done.29 = bf16[8,64,512]{2,1,0:T(8,128)(2,1)S(1)} collective-permute-done((bf16[8,64,512]{2,1,0:T(8,128)(2,1)S(1)}, bf16[8,64,512]{2,1,0:T(8,128)(2,1)S(1)}, u32[]{:S(2)}, u32[]{:S(2)}) %collective-permute-start.29) | collective-permute-done | bytes 524320 | tf_op jit(solution)/shard_map/ppermute | solution.py:119
  203.9 12.0 %collective-permute-done.34 = f32[56,512]{1,0:T(8,128)S(1)} collective-permute-done((f32[56,512]{1,0:T(8,128)S(1)}, f32[56,512]{1,0:T(8,128)S(1)}, u32[]{:S(2)}, u32[]{:S(2)}) %collective-permute-start.34) | collective-permute-done | bytes 114720 | tf_op jit(solution)/shard_map/ppermute | solution.py:119
  219.3 5.0 %collective-permute-done.38 = f32[56,512]{1,0:T(8,128)S(1)} collective-permute-done((f32[56,512]{1,0:T(8,128)S(1)}, f32[56,512]{1,0:T(8,128)S(1)}, u32[]{:S(2)}, u32[]{:S(2)}) %collective-permute-start.38) | collective-permute-done | bytes 114720 | tf_op jit(solution)/shard_map/ppermute | solution.py:119
  224.3 3.0 collective-permute-done.35
  230.5 2.7 collective-permute-start.47
  249.0 10.2 %update_out1.1 = (f32[2,1024,512]{2,1,0:T(8,128)}, f32[2,1024,512]{2,1,0:T(8,128)}, f32[2,1024,512]{2,1,0:T(8,128)}, f32[2,1024,512]{2,1,0:T(8,128)}, f32[8,128]{1,0:T(8,128)}) custom-call(s32[16]{0:T(128)} %broadcast_xor_fusion.spot_ref, bf16[8,128,512]{2,1,0:T(8,128)(2,1)} %copy-done.32, bf16[8,128,512]{2,1,0:T(8,128)(2,1)} %copy-done.34, ...), custom_call_target="tpu_custom_call" | custom-call | tf_op jit(solution)/shard_map/update_out1/pallas_call | solution.py:894
  262.1 10.5 %update_in1.1 = (f32[2,256,2048]{2,1,0:T(8,128)}, f32[2,256,2048]{2,1,0:T(8,128)}, f32[2,256,2048]{2,1,0:T(8,128)}, f32[2,256,2048]{2,1,0:T(8,128)}, f32[8,128]{1,0:T(8,128)}) custom-call(s32[16]{0:T(128)} %broadcast_xor_fusion.spot_ref, bf16[8,128,512]{2,1,0:T(8,128)(2,1)} %copy-done.32, bf16[8,128,512]{2,1,0:T(8,128)(2,1)} %copy-done.34, ...), custom_call_target="tpu_custom_call" | custom-call | tf_op jit(solution)/shard_map/update_in1/pallas_call | solution.py:894
  282.3 14.8 %update_rest.1 = (f32[4,256,512]{2,1,0:T(8,128)}, f32[4,256,512]{2,1,0:T(8,128)}, f32[4,256,512]{2,1,0:T(8,128)}, f32[3,256,512]{2,1,0:T(8,128)}, f32[256,512]{1...) custom-call(s32[16]{0:T(128)} %broadcast_xor_fusion.spot_ref, ...), custom_call_target="tpu_custom_call" | custom-call | tf_op jit(solution)/shard_map/update_rest/pallas_call | solution.py:1039
  302.5 5.7 %move_layer.2 = (f32[2,256,2048]{2,1,0:T(8,128)}, f32[2,1024,512]{2,1,0:T(8,128)}) custom-call(f32[2]{0:T(128)} %bitcast.34, f32[2,256,2048]{2,1,0:T(8,128)} %w0.4, f32[2,256,2048]{2,1,0:T(8,128)} %get-tuple-element.282.u0, f32[2,1024,512]{2,1,0:T(8,128)} %w1.4, f32[2,1024,512]{2,1,0:T(8,128)} %get-tuple-element.283.u1), custom_call_target="tpu_custom_call", output_to_operand_aliasing={{0}: (2, {}), {1}: (4, {})} | custom-call | tf_op jit(solution)/shard_map/move_layer/pallas_call | solution.py:922
  309.9 5.3 %move_rest.1 = (f32[4,256,512]{2,1,0:T(8,128)}, f32[256,1536]{1,0:T(8,128)}) custom-call(f32[6]{0:T(128)} %get-tuple-element.420.factor_ref, f32[4,256,512]{2,1,0:T(8,128)} %w0.5, f32[4,256,512]{2,1,0:T(8,128)} %get-tuple-element.306.u0, f32[256,1536]{1,0:T(8,128)} %w1.5, ...), custom_call_target="tpu_custom_call", output_to_operand_aliasing={{0}: (2, {}), {1}: (4, {})} | custom-call | tf_op jit(solution)/shard_map/move_rest/pallas_call | solution.py:946
  317.6 10.2 %update_out0.1 = (f32[2,1024,512]{2,1,0:T(8,128)}, f32[2,1024,512]{2,1,0:T(8,128)}, f32[2,1024,512]{2,1,0:T(8,128)}, f32[2,1024,512]{2,1,0:T(8,128)}, f32[8,128]{1,0:T(8,128)}) custom-call(s32[16]{0:T(128)} %broadcast_xor_fusion.spot_ref, bf16[8,128,512]{2,1,0:T(8,128)(2,1)} %copy-done.33, ...), custom_call_target="tpu_custom_call", output_to_operand_aliasing={{0}: (8, {}), {1}: (9, {}), {2}: (10, {}), {3}: (11, {})} | custom-call | tf_op jit(solution)/shard_map/update_out0/pallas_call | solution.py:894
  328.5 10.3 %update_in0.1 = (f32[2,256,2048]{2,1,0:T(8,128)}, f32[2,256,2048]{2,1,0:T(8,128)}, f32[2,256,2048]{2,1,0:T(8,128)}, f32[2,256,2048]{2,1,0:T(8,128)}, f32[8,128]{1,0:T(8,128)}) custom-call(s32[16]{0:T(128)} %broadcast_xor_fusion.spot_ref, bf16[8,128,512]{2,1,0:T(8,128)(2,1)} %copy-done.33, ...), custom_call_target="tpu_custom_call", output_to_operand_aliasing={{0}: (8, {}), {1}: (9, {}), {2}: (10, {}), {3}: (11, {})} | custom-call | tf_op jit(solution)/shard_map/update_in0/pallas_call | solution.py:894
  347.9 5.7 %move_layer.3 = (f32[2,256,2048]{2,1,0:T(8,128)}, f32[2,1024,512]{2,1,0:T(8,128)}) custom-call(f32[2]{0:T(128)} %get-tuple-element.414.factor_ref, f32[2,256,2048]{2,1,0:T(8,128)} %w0.4, f32[2,256,2048]{2,1,0:T(8,128)} %get-tuple-element.296.u0, f32[2,1024,512]{2,1,0:T(8,128)} %w1.4, ...), custom_call_target="tpu_custom_call", output_to_operand_aliasing={{0}: (2, {}), {1}: (4, {})} | custom-call | tf_op jit(solution)/shard_map/move_layer/pallas_call | solution.py:922
  (298 shorter events, 116.7 us)
Async XLA Ops:
  3.4 17.6 %collective-permute-start.1 = (bf16[128,2048]{1,0:T(8,128)(2,1)}, bf16[128,2048]{1,0:T(8,128)(2,1)}, u32[]{:S(2)}, u32[]{:S(2)}) collective-permute-start(bf16[128,2048]{1,0:T(8,128)(2,1)} %bitcast.43), channel_id=1, source_target_pairs={{0,1},{1,0},{2,3},{3,2},{4,5},{5,4},{6,7},{7,6},{8,9},{9,8},{10,11... | collective-permute-start | bytes 1572872 | tf_op jit(solution)/shard_map/ppermute | solution.py:119
  6.4 14.6 %collective-permute-start = (bf16[37,256]{1,0:T(8,128)(2,1)S(1)}, bf16[37,256]{1,0:T(8,128)(2,1)S(1)}, u32[]{:S(2)}, u32[]{:S(2)}) collective-permute-start(bf16[37,256]{1,0:T(8,128)(2,1)S(1)} %convert_element_type.322), channel_id=1, source_target_pairs={{0,1},{1,0},{2,3},{3,2},{4,5},{5,4},{6,7},{7,6},{8,9},{9,8},{10,11... | collective-permute-start | bytes 56840 | tf_op jit(solution)/shard_map/ppermute | solution.py:119
  21.1 14.9 %collective-permute-start.3 = (bf16[512,512]{1,0:T(8,128)(2,1)}, bf16[512,512]{1,0:T(8,128)(2,1)}, u32[]{:S(2)}, u32[]{:S(2)}) collective-permute-start(bf16[512,512]{1,0:T(8,128)(2,1)} %bitcast.42), channel_id=1, source_target_pairs={{0,1},{1,0},{2,3},{3,2},{4,5},{5,4},{6,7},{7,6},{8,9},{9,8},{10,11... | collective-permute-start | bytes 1572872 | tf_op jit(solution)/shard_map/ppermute | solution.py:119
  35.9 13.7 %collective-permute-start.4 = (bf16[4,128,512]{2,1,0:T(8,128)(2,1)S(1)}, bf16[4,128,512]{2,1,0:T(8,128)(2,1)}, u32[]{:S(2)}, u32[]{:S(2)}) collective-permute-start(bf16[4,128,512]{2,1,0:T(8,128)(2,1)S(1)} %copy-done.30), channel_id=1, source_target_pairs={{0,1},{1,0},{2,3},{3,2},{4,5},{5,4},{6,7},{7,6},{8,9},{9,8},{10,11... | collective-permute-start | bytes 1572872 | tf_op jit(solution)/shard_map/ppermute | solution.py:119
  37.7 15.2 %collective-permute-start.5 = (bf16[512,512]{1,0:T(8,128)(2,1)}, bf16[512,512]{1,0:T(8,128)(2,1)}, u32[]{:S(2)}, u32[]{:S(2)}) collective-permute-start(bf16[512,512]{1,0:T(8,128)(2,1)} %collective-permute-done.3.rest_1_), channel_id=1, source_target_pairs={{0,2},{2,0},{4,6},{6,4},{8,10},{10,8},{12,14},{14,12},{16,18},{18,... | collective-permute-start | bytes 1572872 | tf_op jit(solution)/shard_map/ppermute | solution.py:119
  50.5 20.1 %collective-permute-start.7 = (bf16[128,1536]{1,0:T(8,128)(2,1)}, bf16[128,1536]{1,0:T(8,128)(2,1)S(1)}, u32[]{:S(2)}, u32[]{:S(2)}) collective-permute-start(bf16[128,1536]{1,0:T(8,128)(2,1)} %copy-done.31), channel_id=1, source_target_pairs={{0,1},{1,0},{2,3},{3,2},{4,5},{5,4},{6,7},{7,6},{8,9},{9,8},{10,11... | collective-permute-start | bytes 1179656 | tf_op jit(solution)/shard_map/ppermute | solution.py:119
  52.3 25.8 %collective-permute-start.9 = (bf16[128,2048]{1,0:T(8,128)(2,1)}, bf16[128,2048]{1,0:T(8,128)(2,1)S(1)}, u32[]{:S(2)}, u32[]{:S(2)}) collective-permute-start(bf16[128,2048]{1,0:T(8,128)(2,1)} %copy-done.28), channel_id=1, source_target_pairs={{0,1},{1,0},{2,3},{3,2},{4,5},{5,4},{6,7},{7,6},{8,9},{9,8},{10,11... | collective-permute-start | bytes 1572872 | tf_op jit(solution)/shard_map/ppermute | solution.py:119
  69.0 15.8 %collective-permute-start.11 = (bf16[512,512]{1,0:T(8,128)(2,1)S(1)}, bf16[512,512]{1,0:T(8,128)(2,1)S(1)}, u32[]{:S(2)}, u32[]{:S(2)}) collective-permute-start(bf16[512,512]{1,0:T(8,128)(2,1)S(1)} %copy-done.27), channel_id=1, source_target_pairs={{0,1},{1,0},{2,3},{3,2},{4,5},{5,4},{6,7},{7,6},{8,9},{9,8},{10,11... | collective-permute-start | bytes 1572872 | tf_op jit(solution)/shard_map/ppermute | solution.py:119
  97.1 15.9 %collective-permute-start.13 = (bf16[16,128,512]{2,1,0:T(8,128)(2,1)S(1)}, bf16[16,128,512]{2,1,0:T(8,128)(2,1)S(1)}, u32[]{:S(2)}, u32[]{:S(2)}) collective-permute-start(bf16[16,128,512]{2,1,0:T(8,128)(2,1)S(1)} %get-tuple-element.203), channel_id=1, source_target_pairs={{0,2},{2,0},{4,6},{6,4},{8,10},{10,8},{12,14},{14,12},{16,18},{18,... | collective-permute-start | bytes 6291464 | tf_op jit(solution)/shard_map/ppermute | solution.py:119
  112.6 31.1 %collective-permute-start.15 = (bf16[16,48,512]{2,1,0:T(8,128)(2,1)S(1)}, bf16[16,48,512]{2,1,0:T(8,128)(2,1)S(1)}, u32[]{:S(2)}, u32[]{:S(2)}) collective-permute-start(bf16[16,48,512]{2,1,0:T(8,128)(2,1)S(1)} %get-tuple-element.214), channel_id=1, source_target_pairs={{0,2},{2,0},{4,6},{6,4},{8,10},{10,8},{12,14},{14,12},{16,18},{18,... | collective-permute-start | bytes 2359304 | tf_op jit(solution)/shard_map/ppermute | solution.py:119
  113.7 30.8 %collective-permute-start.14 = (bf16[8,128,512]{2,1,0:T(8,128)(2,1)S(1)}, bf16[8,128,512]{2,1,0:T(8,128)(2,1)S(1)}, u32[]{:S(2)}, u32[]{:S(2)}) collective-permute-start(bf16[8,128,512]{2,1,0:T(8,128)(2,1)S(1)} %get-tuple-element.381), channel_id=1, source_target_pairs={{0,1},{1,0},{2,3},{3,2},{4,5},{5,4},{6,7},{7,6},{8,9},{9,8},{10,11... | collective-permute-start | bytes 3145736 | tf_op jit(solution)/shard_map/ppermute | solution.py:119
  143.9 12.1 %collective-permute-start.18 = (bf16[8,48,512]{2,1,0:T(8,128)(2,1)S(1)}, bf16[8,48,512]{2,1,0:T(8,128)(2,1)S(1)}, u32[]{:S(2)}, u32[]{:S(2)}) collective-permute-start(bf16[8,48,512]{2,1,0:T(8,128)(2,1)S(1)} %get-tuple-element.391), channel_id=1, source_target_pairs={{0,1},{1,0},{2,3},{3,2},{4,5},{5,4},{6,7},{7,6},{8,9},{9,8},{10,11... | collective-permute-start | bytes 1179656 | tf_op jit(solution)/shard_map/ppermute | solution.py:119
  144.9 14.1 %collective-permute-start.16 = (bf16[4,128,512]{2,1,0:T(8,128)(2,1)S(1)}, bf16[4,128,512]{2,1,0:T(8,128)(2,1)S(1)}, u32[]{:S(2)}, u32[]{:S(2)}) collective-permute-start(bf16[4,128,512]{2,1,0:T(8,128)(2,1)S(1)} %get-tuple-element.389), channel_id=1, source_target_pairs={{0,4},{2,6},{4,0},{6,2},{8,12},{10,14},{12,8},{14,10},{16,20},{18,... | collective-permute-start | bytes 1572872 | tf_op jit(solution)/shard_map/ppermute | solution.py:119
  150.6 16.2 %collective-permute-start.19 = (bf16[8,64,512]{2,1,0:T(8,128)(2,1)S(1)}, bf16[8,64,512]{2,1,0:T(8,128)(2,1)S(1)}, u32[]{:S(2)}, u32[]{:S(2)}) collective-permute-start(bf16[8,64,512]{2,1,0:T(8,128)(2,1)S(1)} %get-tuple-element.387), channel_id=1, source_target_pairs={{0,1},{1,0},{2,3},{3,2},{4,5},{5,4},{6,7},{7,6},{8,9},{9,8},{10,11... | collective-permute-start | bytes 1572872 | tf_op jit(solution)/shard_map/ppermute | solution.py:119
  152.1 14.9 %collective-permute-start.21 = (bf16[16,64,512]{2,1,0:T(8,128)(2,1)S(1)}, bf16[16,64,512]{2,1,0:T(8,128)(2,1)S(1)}, u32[]{:S(2)}, u32[]{:S(2)}) collective-permute-start(bf16[16,64,512]{2,1,0:T(8,128)(2,1)S(1)} %get-tuple-element.232), channel_id=1, source_target_pairs={{0,2},{2,0},{4,6},{6,4},{8,10},{10,8},{12,14},{14,12},{16,18},{18,... | collective-permute-start | bytes 3145736 | tf_op jit(solution)/shard_map/ppermute | solution.py:119
  167.4 13.1 %collective-permute-start.24 = (bf16[16,64,512]{2,1,0:T(8,128)(2,1)S(1)}, bf16[16,64,512]{2,1,0:T(8,128)(2,1)S(1)}, u32[]{:S(2)}, u32[]{:S(2)}) collective-permute-start(bf16[16,64,512]{2,1,0:T(8,128)(2,1)S(1)} %get-tuple-element.248), channel_id=1, source_target_pairs={{0,2},{2,0},{4,6},{6,4},{8,10},{10,8},{12,14},{14,12},{16,18},{18,... | collective-permute-start | bytes 3145736 | tf_op jit(solution)/shard_map/ppermute | solution.py:119
  167.4 12.9 %collective-permute-start.22 = (bf16[4,112,512]{2,1,0:T(8,128)(2,1)S(1)}, bf16[4,112,512]{2,1,0:T(8,128)(2,1)S(1)}, u32[]{:S(2)}, u32[]{:S(2)}) collective-permute-start(bf16[4,112,512]{2,1,0:T(8,128)(2,1)S(1)} %pad_maximum_fusion.3), channel_id=1, source_target_pairs={{0,4},{2,6},{4,0},{6,2},{8,12},{10,14},{12,8},{14,10},{16,20},{18,... | collective-permute-start | bytes 1376264 | tf_op jit(solution)/shard_map/ppermute | solution.py:119
  171.6 15.5 %collective-permute-start.28 = (bf16[8,64,512]{2,1,0:T(8,128)(2,1)S(1)}, bf16[8,64,512]{2,1,0:T(8,128)(2,1)S(1)}, u32[]{:S(2)}, u32[]{:S(2)}) collective-permute-start(bf16[8,64,512]{2,1,0:T(8,128)(2,1)S(1)} %get-tuple-element.252), channel_id=1, source_target_pairs={{0,1},{1,0},{2,3},{3,2},{4,5},{5,4},{6,7},{7,6},{8,9},{9,8},{10,11... | collective-permute-start | bytes 1572872 | tf_op jit(solution)/shard_map/ppermute | solution.py:119
  182.2 17.4 %collective-permute-start.29 = (bf16[8,64,512]{2,1,0:T(8,128)(2,1)S(1)}, bf16[8,64,512]{2,1,0:T(8,128)(2,1)S(1)}, u32[]{:S(2)}, u32[]{:S(2)}) collective-permute-start(bf16[8,64,512]{2,1,0:T(8,128)(2,1)S(1)} %get-tuple-element.253), channel_id=1, source_target_pairs={{0,1},{1,0},{2,3},{3,2},{4,5},{5,4},{6,7},{7,6},{8,9},{9,8},{10,11... | collective-permute-start | bytes 1572872 | tf_op jit(solution)/shard_map/ppermute | solution.py:119
  199.9 16.2 %collective-permute-start.33 = (bf16[4,128,512]{2,1,0:T(8,128)(2,1)S(1)}, bf16[4,128,512]{2,1,0:T(8,128)(2,1)S(1)}, u32[]{:S(2)}, u32[]{:S(2)}) collective-permute-start(bf16[4,128,512]{2,1,0:T(8,128)(2,1)S(1)} %pad_maximum_fusion.1), channel_id=1, source_target_pairs={{0,4},{2,6},{4,0},{6,2},{8,12},{10,14},{12,8},{14,10},{16,20},{18,... | collective-permute-start | bytes 1572872 | tf_op jit(solution)/shard_map/ppermute | solution.py:119
  200.4 15.4 %collective-permute-start.34 = (f32[56,512]{1,0:T(8,128)S(1)}, f32[56,512]{1,0:T(8,128)S(1)}, u32[]{:S(2)}, u32[]{:S(2)}) collective-permute-start(f32[56,512]{1,0:T(8,128)S(1)} %add.229), channel_id=1, source_target_pairs={{0,4},{2,6},{4,0},{6,2},{8,12},{10,14},{12,8},{14,10},{16,20},{18,... | collective-permute-start | bytes 344072 | tf_op jit(solution)/shard_map/ppermute | solution.py:119
  201.9 13.9 %collective-permute-start.31 = (bf16[1,112,512]{2,1,0:T(8,128)(2,1)}, bf16[1,112,512]{2,1,0:T(8,128)(2,1)S(1)}, u32[]{:S(2)}, u32[]{:S(2)}) collective-permute-start(bf16[1,112,512]{2,1,0:T(8,128)(2,1)} %add_convert_fusion.33), channel_id=1, source_target_pairs={{0,16},{2,18},{4,20},{6,22},{8,24},{10,26},{12,28},{14,30},{16,0},... | collective-permute-start | bytes 344072 | tf_op jit(solution)/shard_map/ppermute | solution.py:119
  202.3 13.7 %collective-permute-start.32 = (bf16[2,128,512]{2,1,0:T(8,128)(2,1)S(1)}, bf16[2,128,512]{2,1,0:T(8,128)(2,1)S(1)}, u32[]{:S(2)}, u32[]{:S(2)}) collective-permute-start(bf16[2,128,512]{2,1,0:T(8,128)(2,1)S(1)} %pad_maximum_fusion.6), channel_id=1, source_target_pairs={{0,8},{2,10},{4,12},{6,14},{8,0},{10,2},{12,4},{14,6},{16,24},{18,... | collective-permute-start | bytes 786440 | tf_op jit(solution)/shard_map/ppermute | solution.py:119
  218.4 12.0 %collective-permute-start.36 = (bf16[4,128,512]{2,1,0:T(8,128)(2,1)S(1)}, bf16[4,128,512]{2,1,0:T(8,128)(2,1)S(1)}, u32[]{:S(2)}, u32[]{:S(2)}) collective-permute-start(bf16[4,128,512]{2,1,0:T(8,128)(2,1)S(1)} %pad_maximum_fusion.2), channel_id=1, source_target_pairs={{0,4},{2,6},{4,0},{6,2},{8,12},{10,14},{12,8},{14,10},{16,20},{18,... | collective-permute-start | bytes 1572872 | tf_op jit(solution)/shard_map/ppermute | solution.py:119
  236.0 12.1 %collective-permute-start.41 = (bf16[8,128,512]{2,1,0:T(8,128)(2,1)S(1)}, bf16[8,128,512]{2,1,0:T(8,128)(2,1)S(1)}, u32[]{:S(2)}, u32[]{:S(2)}) collective-permute-start(bf16[8,128,512]{2,1,0:T(8,128)(2,1)S(1)} %pad_maximum_fusion.g0_near.g1_near), channel_id=1, source_target_pairs={{0,2},{2,0},{4,6},{6,4},{8,10},{10,8},{12,14},{14,12},{16,18},{18,... | collective-permute-start | bytes 3145736 | tf_op jit(solution)/shard_map/ppermute | solution.py:119
  236.3 11.0 %collective-permute-start.39 = (bf16[2,112,512]{2,1,0:T(8,128)(2,1)}, bf16[2,112,512]{2,1,0:T(8,128)(2,1)S(1)}, u32[]{:S(2)}, u32[]{:S(2)}) collective-permute-start(bf16[2,112,512]{2,1,0:T(8,128)(2,1)} %pad_maximum_fusion.8), channel_id=1, source_target_pairs={{0,8},{2,10},{4,12},{6,14},{8,0},{10,2},{12,4},{14,6},{16,24},{18,... | collective-permute-start | bytes 688136 | tf_op jit(solution)/shard_map/ppermute | solution.py:119
  245.8 13.5 %collective-permute-start.43 = (bf16[1,128,512]{2,1,0:T(8,128)(2,1)S(1)}, bf16[1,128,512]{2,1,0:T(8,128)(2,1)}, u32[]{:S(2)}, u32[]{:S(2)}) collective-permute-start(bf16[1,128,512]{2,1,0:T(8,128)(2,1)S(1)} %add_convert_fusion.26), channel_id=1, source_target_pairs={{0,16},{2,18},{4,20},{6,22},{8,24},{10,26},{12,28},{14,30},{16,0},... | collective-permute-start | bytes 393224 | tf_op jit(solution)/shard_map/ppermute | solution.py:119
  247.3 14.0 %collective-permute-start.42 = (bf16[4,112,512]{2,1,0:T(8,128)(2,1)S(1)}, bf16[4,112,512]{2,1,0:T(8,128)(2,1)S(1)}, u32[]{:S(2)}, u32[]{:S(2)}) collective-permute-start(bf16[4,112,512]{2,1,0:T(8,128)(2,1)S(1)} %pad_maximum_fusion.4), channel_id=1, source_target_pairs={{0,4},{2,6},{4,0},{6,2},{8,12},{10,14},{12,8},{14,10},{16,20},{18,... | collective-permute-start | bytes 1376264 | tf_op jit(solution)/shard_map/ppermute | solution.py:119
  260.2 12.4 %collective-permute-start.44 = (bf16[2,128,512]{2,1,0:T(8,128)(2,1)S(1)}, bf16[2,128,512]{2,1,0:T(8,128)(2,1)S(1)}, u32[]{:S(2)}, u32[]{:S(2)}) collective-permute-start(bf16[2,128,512]{2,1,0:T(8,128)(2,1)S(1)} %constant_dynamic-update-slice_fusion.2), channel_id=1, source_target_pairs={{0,8},{2,10},{4,12},{6,14},{8,0},{10,2},{12,4},{14,6},{16,24},{18,... | collective-permute-start | bytes 786440 | tf_op jit(solution)/shard_map/ppermute | solution.py:119
  261.3 20.0 %collective-permute-start.45 = (bf16[8,112,512]{2,1,0:T(8,128)(2,1)S(1)}, bf16[8,112,512]{2,1,0:T(8,128)(2,1)S(1)}, u32[]{:S(2)}, u32[]{:S(2)}) collective-permute-start(bf16[8,112,512]{2,1,0:T(8,128)(2,1)S(1)} %constant_dynamic-update-slice_fusion.g0_near.g1_near), channel_id=1, source_target_pairs={{0,2},{2,0},{4,6},{6,4},{8,10},{10,8},{12,14},{14,12},{16,18},{18,... | collective-permute-start | bytes 2752520 | tf_op jit(solution)/shard_map/ppermute | solution.py:119
  272.7 24.5 %collective-permute-start.46 = (bf16[4,128,512]{2,1,0:T(8,128)(2,1)S(1)}, bf16[4,128,512]{2,1,0:T(8,128)(2,1)S(1)}, u32[]{:S(2)}, u32[]{:S(2)}) collective-permute-start(bf16[4,128,512]{2,1,0:T(8,128)(2,1)S(1)} %constant_dynamic-update-slice_fusion.4), channel_id=1, source_target_pairs={{0,4},{2,6},{4,0},{6,2},{8,12},{10,14},{12,8},{14,10},{16,20},{18,... | collective-permute-start | bytes 1572872 | tf_op jit(solution)/shard_map/ppermute | solution.py:119
  297.2 19.3 %collective-permute-start.49 = (bf16[8,128,512]{2,1,0:T(8,128)(2,1)S(1)}, bf16[8,128,512]{2,1,0:T(8,128)(2,1)S(1)}, u32[]{:S(2)}, u32[]{:S(2)}) collective-permute-start(bf16[8,128,512]{2,1,0:T(8,128)(2,1)S(1)} %constant_dynamic-update-slice_fusion.6.g0_near.g1_near), channel_id=1, source_target_pairs={{0,2},{2,0},{4,6},{6,4},{8,10},{10,8},{12,14},{14,12},{16,18},{18,... | collective-permute-start | bytes 3145736 | tf_op jit(solution)/shard_map/ppermute | solution.py:119
  (71 other events, 575.7 us)
where the time goes:
time: 359 us; the launch traced here: 354 us
  Pallas kernels  163 us (45%)
  waiting for transfers between devices  80.9 us (23%)
  starting transfers between devices  49.3 us (14%)
  local copies, waits for them, and re-layouts  40.1 us (11%)
  other arithmetic  17.4 us (5%)
  between operations  3.82 us (1%)
    pallas_call x11, Pallas kernels, call(): pl.pallas_call(kernel, out_shape=list(outs), in_specs=specs, out_specs=[v...  87.5 us
    ppermute x51, waiting for transfers between devices, swap(): return lax.ppermute(values, axis, [(i, i ^ 1 << bit) for i in range(count)])  80.9 us
    ppermute x51, starting transfers between devices, swap(): return lax.ppermute(values, axis, [(i, i ^ 1 << bit) for i in range(count)])  49.3 us
    pallas_call x4, Pallas kernels, update_matrix(): pl.pallas_call(kernel, out_shape=[shape(states[0].shape, f32)] * 4 + [sha...  41.2 us
    unnamed x119, local copies, waits for them, and re-layouts  31.3 us
    pallas_call x1, Pallas kernels, update_rest(): pl.pallas_call(kernel, out_shape=[shape(attn[0].shape, f32)] * 3 + [shape...  14.8 us
    pallas_call x2, Pallas kernels, move_layer(): pl.pallas_call(kernel, out_shape=[shape(win.shape, f32), shape(wout.shape...  11.4 us
  transfers between devices with their start and end apart: 51, of which 22 were waited for; matrix products, arithmetic and copies ran while one was open for 7% of the time, Pallas kernels for 35%

commit v1 on v0

--- a/solution.py
+++ b/solution.py
@@ -331,16 +331,16 @@
             whole_ref[k, pl.ds(third, half), :] = far[k]
 
 
-def put(out_refs, plan, place_ref, value, row, rows_each, first):
+def put(out_refs, plan, place_ref, value, row, rows_each, first, shift=0):
     kept_ref, sent_ref = out_refs
     low = value.astype(bf16)
-    core, mine = place_ref[1] == 0, place_ref[2]
+    core, mine = place_ref[1] == 0, jnp.bitwise_xor(place_ref[2], shift)
     for k in range(0, value.shape[0] // rows_each, 2):
         even = low[k * rows_each : (k + 1) * rows_each]
         odd = low[(k + 1) * rows_each : (k + 2) * rows_each]
         spot = jnp.bitwise_xor(jnp.int32(plan.place(first + k)), jnp.bitwise_and(mine, PIECES // 2 - 1))
-        kept_ref[spot, row : row + rows_each, :] = jnp.where(core, even, odd)
-        sent_ref[spot, row : row + rows_each, :] = jnp.where(core, odd, even)
+        kept_ref[spot, pl.ds(row, rows_each), :] = jnp.where(core, even, odd)
+        sent_ref[spot, pl.ds(row, rows_each), :] = jnp.where(core, odd, even)
 
 
 def halves(rows):
@@ -359,34 +359,41 @@
     )(*ins)
 
 
-def ffn_ahead(values, gain, win, wout, entry_ref, hidden_ref, slope_ref):
+def ffn_ahead(values, gain, win, wout, entry_ref, hidden_ref, slope_ref, sum_ref):
     normed, _ = stats(values)
-    entry = (normed * gain).astype(bf16)
-    entry_ref[...] = entry
-    total = jnp.zeros(values.shape, f32)
-    for b in range(FF // D):
-        cols = slice(b * D, (b + 1) * D)
-        before = dot(entry, win[:, cols])
+    entry_ref[...] = (normed * gain).astype(bf16)
+    sum_ref[...] = jnp.zeros_like(sum_ref)
+
+    def step(b, carry):
+        cols = pl.ds(pl.multiple_of(b * D, D), D)
+        before = dot(entry_ref[...], win[:, cols])
         sig = logistic(before)
         hidden = (before * sig).astype(bf16)
         hidden_ref[:, cols] = hidden
         slope_ref[:, cols] = slope_of(before, sig).astype(bf16)
-        total = total + dot(hidden, wout[cols, :])
-    return total
-
-
-def ffn_behind(grad, values, gain, win, wout, entry_ref, hidden_ref, slope_ref, out_refs, plan, place_ref):
+        sum_ref[...] += dot(hidden, wout[cols, :])
+        return carry
+
+    lax.fori_loop(0, FF // D, step, 0)
+    return sum_ref[...]
+
+
+def ffn_behind(grad, values, gain, win, wout, entry_ref, hidden_ref, slope_ref, sum_ref, out_refs, plan, place_ref):
     normed, scale = stats(values)
-    entry = entry_ref[...]
     branch = (0.5 * grad).astype(bf16)
-    grad_entry = jnp.zeros(values.shape, f32)
-    for b in range(FF // D):
-        cols = slice(b * D, (b + 1) * D)
-        put(out_refs, plan, place_ref, dot_rows(hidden_ref[:, cols], branch), 64, 64, 8 * b)
+    sum_ref[...] = jnp.zeros_like(sum_ref)
+
+    def step(b, carry):
+        cols = pl.ds(pl.multiple_of(b * D, D), D)
+        shift = jnp.bitwise_xor((b % 2) * plan.place(8), (b // 2) * plan.place(16))
+        put(out_refs, plan, place_ref, dot_rows(hidden_ref[:, cols], branch), 64, 64, 0, shift)
         grad_before = (dot_cols(branch, wout[cols, :]) * slope_ref[:, cols].astype(f32)).astype(bf16)
-        put(out_refs, plan, place_ref, dot_rows(entry, grad_before), 16 * b, 16, 0)
-        grad_entry = grad_entry + dot_cols(grad_before, win[:, cols])
-    back, grad_gain = norm_back(grad_entry, normed, scale, gain)
+        put(out_refs, plan, place_ref, dot_rows(entry_ref[...], grad_before), pl.multiple_of(16 * b, 16), 16, 0)
+        sum_ref[...] += dot_cols(grad_before, win[:, cols])
+        return carry
+
+    lax.fori_loop(0, FF // D, step, 0)
+    back, grad_gain = norm_back(sum_ref[...], normed, scale, gain)
     return grad + back, grad_gain
 
 
@@ -401,12 +408,16 @@
         entry = (normed * vec_ref[31:32, :]).astype(bf16)
         entry_ref[...] = entry
         join(place_ref, wins, win)
-        for b in range(FF // D):
-            cols = slice(b * D, (b + 1) * D)
-            before = dot(entry, win[:, cols])
+
+        def step(b, carry):
+            cols = pl.ds(pl.multiple_of(b * D, D), D)
+            before = dot(entry_ref[...], win[:, cols])
             sig = logistic(before)
             hidden_ref[:, cols] = (before * sig).astype(bf16)
             slope_ref[:, cols] = slope_of(before, sig).astype(bf16)
+            return carry
+
+        lax.fori_loop(0, FF // D, step, 0)
 
     return call(
         kernel,
@@ -446,12 +457,12 @@
     def kernel(place_ref, len_ref, x_ref, vec_ref, cot_ref, *rest):
         wins, wouts = rest[:n], rest[n : 2 * n]
         y_ref, dx_ref, gain_ref, *g_refs = rest[2 * n : 2 * n + 5]
-        win, wout, entry_ref, hidden_ref, slope_ref = rest[2 * n + 5 :]
+        win, wout, entry_ref, hidden_ref, slope_ref, sum_ref = rest[2 * n + 5 :]
         join(place_ref, wins, win)
         join(place_ref, wouts, wout)
         x = x_ref[...]
         gain = vec_ref[35:36, :]
-        total = ffn_ahead(x, gain, win, wout, entry_ref, hidden_ref, slope_ref)
+        total = ffn_ahead(x, gain, win, wout, entry_ref, hidden_ref, slope_ref, sum_ref)
         normed, scale = stats(x + 0.5 * total)
         top = vec_ref[36:37, :]
         y_ref[...] = (normed * top).astype(bf16)
@@ -463,7 +474,7 @@
             grads.append(jnp.where(spot < len_ref[s], part, 0.0))
         back, grad_top = norm_back(jnp.concatenate(grads, axis=0), normed, scale, top)
         grad, grad_gain = ffn_behind(
-            back, x, gain, win, wout, entry_ref, hidden_ref, slope_ref, g_refs, plan, place_ref
+            back, x, gain, win, wout, entry_ref, hidden_ref, slope_ref, sum_ref, g_refs, plan, place_ref
         )
         dx_ref[...] = grad
         gain_ref[...] = jnp.concatenate([grad_gain, grad_top, jnp.zeros((6, D), f32)], axis=0)
@@ -479,6 +490,7 @@
             pltpu.VMEM((rows, D), bf16),
             pltpu.VMEM((rows, FF), bf16),
             pltpu.VMEM((rows, FF), bf16),
+            pltpu.VMEM((rows, D), f32),
         ],
         "ffn_last",
     )
@@ -494,11 +506,16 @@
         (wout,) = rest[n + 3 :]
         join(place_ref, wouts, wout)
         branch = (0.5 * grad_ref[...]).astype(bf16)
-        for b in range(FF // D):
-            cols = slice(b * D, (b + 1) * D)
-            put(g_refs, plan, place_ref, dot_rows(hidden_ref[:, cols], branch), 0, 64, 8 * b)
+
+        def step(b, carry):
+            cols = pl.ds(pl.multiple_of(b * D, D), D)
+            shift = jnp.bitwise_xor((b % 2) * plan.place(8), (b // 2) * plan.place(16))
+            put(g_refs, plan, place_ref, dot_rows(hidden_ref[:, cols], branch), 0, 64, 0, shift)
             spread = dot_cols(branch, wout[cols, :])
             before_ref[:, cols] = (spread * slope_ref[:, cols].astype(f32)).astype(bf16)
+            return carry
+
+        lax.fori_loop(0, FF // D, step, 0)
 
     return call(
         kernel,
@@ -517,16 +534,21 @@
     def kernel(place_ref, grad_ref, x_ref, vec_ref, entry_ref, before_ref, *rest):
         wins = rest[:n]
         dx_ref, gain_ref, *g_refs = rest[n : n + 4]
-        (win,) = rest[n + 4 :]
+        win, sum_ref = rest[n + 4 :]
         join(place_ref, wins, win)
         low = entry_ref[...]
-        grad_entry = jnp.zeros((rows, D), f32)
-        for b in range(FF // D):
-            cols = slice(b * D, (b + 1) * D)
-            put(g_refs, plan, place_ref, dot_rows(low, before_ref[:, cols]), 16 * b, 16, 0)
-            grad_entry = grad_entry + dot_cols(before_ref[:, cols], win[:, cols])
+        sum_ref[...] = jnp.zeros_like(sum_ref)
+
+        def step(b, carry):
+            cols = pl.ds(pl.multiple_of(b * D, D), D)
+            low_row = pl.multiple_of(16 * b, 16)
+            put(g_refs, plan, place_ref, dot_rows(low, before_ref[:, cols]), low_row, 16, 0)
+            sum_ref[...] += dot_cols(before_ref[:, cols], win[:, cols])
+            return carry
+
+        lax.fori_loop(0, FF // D, step, 0)
         normed, scale = stats(x_ref[...].astype(f32))
-        back, grad_gain = norm_back(grad_entry, normed, scale, vec_ref[31:32, :])
+        back, grad_gain = norm_back(sum_ref[...], normed, scale, vec_ref[31:32, :])
         dx_ref[...] = (grad_ref[...] + back).astype(bf16)
         gain_ref[...] = jnp.concatenate([grad_gain, jnp.zeros((7, D), f32)], axis=0)
 
@@ -535,7 +557,7 @@
         [shape((rows, D), bf16), shape((8, D), f32), *halves(64)],
         [place, grad, frames, vec, entry, before, *win_parts],
         [smem()] + [vmem()] * 5 + [vmem()] * n,
-        [pltpu.VMEM((D, FF), bf16)],
+        [pltpu.VMEM((D, FF), bf16), pltpu.VMEM((rows, D), f32)],
         "ffn_first_in",
     )
 
@@ -1209,7 +1231,9 @@
     vec_grad = lax.dynamic_slice(small, (0, shard * wide), (KERNEL + 6, wide))
     rel_grad = jnp.concatenate([small[40:56, b * HEAD : (b + 1) * HEAD] for b in range(5)], axis=0)[:RELS]
     vec_m, vec_q, vec_up = adam(vectors, vectors_moment, vectors_square, vec_grad)
-    rel_m, rel_q, rel_up = adam(rel_keys, rel_moment, rel_square, rel_grad)
+    rel_m, rel_q, rel_up = (
+        v.T for v in adam(rel_keys.T, rel_moment.T, rel_square.T, rel_grad.T)
+    )
 
     vec_sums = []
     for part in (vectors, vec_up):
@@ -1233,7 +1257,7 @@
         0, first.kept, 1, spots, in_states, half_in, "update_in0"
     )
     final = sum_shards(jnp.sum(jnp.concatenate([sums_in0[:2], sums_out0[:2]], axis=0), axis=1), plan)
-    rel_sums = jnp.stack([jnp.sum(rel_keys * rel_keys), jnp.sum(rel_up * rel_up)])
+    rel_sums = jnp.stack([jnp.sum(rel_keys.T * rel_keys.T), jnp.sum(rel_up.T * rel_up.T)])
     late_ratio = ratio_of(rel_sums)
     final_ratio = ratio_of(final)
 
@@ -1277,7 +1301,7 @@
         vec_m,
         vec_q,
         rel_grad,
-        move(rel_keys, rel_up, late_ratio[2][0]),
+        move(rel_keys.T, rel_up.T, late_ratio[2][0]).T,
         rel_m,
         rel_q,
         trust_norms,

time: 359 us -> 351 us (0.978)
  waiting for transfers between devices: 80.9 us -> 89.1 us
  local copies, waits for them, and re-layouts: 40.1 us -> 35.7 us
  starting transfers between devices: 49.3 us -> 44.9 us
  Pallas kernels: 163 us -> 159 us
    ppermute x51, waiting for transfers between devices: 80.9 us -> 89.1 us  [swap(): return lax.ppermute(values, axis, [(i, i ^ 1 << bit) for i in range(count)])]
    ppermute x51, starting transfers between devices: 49.3 us -> 44.9 us  [swap(): return lax.ppermute(values, axis, [(i, i ^ 1 << bit) for i in range(count)])]
    unnamed x119 -> x113, local copies, waits for them, and re-layouts: 31.3 us -> 27.6 us
    pallas_call x11, Pallas kernels: 87.5 us -> 83.8 us  [call(): pl.pallas_call(kernel, out_shape=list(outs), in_specs=specs, out_specs=[v...]
  transfers between devices with their start and end apart: 51 -> 51, of which waited for: 22 -> 24; matrix products, arithmetic and copies ran while one was open for 7% -> 6% of each run, Pallas kernels for 35% -> 34%
where the time goes in v1:
time: 351 us; the launch traced here: 349 us
  Pallas kernels  159 us (45%)
  waiting for transfers between devices  89.1 us (25%)
  starting transfers between devices  44.9 us (13%)
  local copies, waits for them, and re-layouts  35.7 us (10%)
  other arithmetic  16.9 us (5%)
  between operations  3.63 us (1%)
    ppermute x51, waiting for transfers between devices, swap(): return lax.ppermute(values, axis, [(i, i ^ 1 << bit) for i in range(count)])  89.1 us
    pallas_call x11, Pallas kernels, call(): pl.pallas_call(kernel, out_shape=list(outs), in_specs=specs, out_specs=[v...  83.8 us
    ppermute x51, starting transfers between devices, swap(): return lax.ppermute(values, axis, [(i, i ^ 1 << bit) for i in range(count)])  44.9 us
    pallas_call x4, Pallas kernels, update_matrix(): pl.pallas_call(kernel, out_shape=[shape(states[0].shape, f32)] * 4 + [sha...  41 us
    unnamed x113, local copies, waits for them, and re-layouts  27.6 us
    pallas_call x1, Pallas kernels, update_rest(): pl.pallas_call(kernel, out_shape=[shape(attn[0].shape, f32)] * 3 + [shape...  14.8 us
    pallas_call x2, Pallas kernels, move_layer(): pl.pallas_call(kernel, out_shape=[shape(win.shape, f32), shape(wout.shape...  11.4 us
  transfers between devices with their start and end apart: 51, of which 24 were waited for; matrix products, arithmetic and copies ran while one was open for 6% of the time, Pallas kernels for 34%

profile of v1, /device:TPU:0, one launch (start us, length us, event | category | flops | bytes accessed | tf_op | source)
XLA Modules:
  0.0 349.3 jit_solution(15891565085791908169)
XLA Ops:
  0.7 2.7 rounded_halves.1
  3.4 3.0 collective-permute-start.1
  26.2 4.5 %ffn_first_up.1 = (bf16[512,512]{1,0:T(8,128)(2,1)S(1)}, bf16[512,2048]{1,0:T(8,128)(2,1)S(1)}, bf16[512,2048]{1,0:T(8,128)(2,1)S(1)}) custom-call(s32[3]{0:T(128)S(1)} %pad_add_fusion.place_ref, bf16[512,512]{1,0:T(8,128)(2,1)S(1)} %bitcast.53, f32[40,512]{1,0:T(8,128)S(1)} %pad_convert_fusion.vec_ref, bf16[256,2048]{1,0:T(8,128)(2,1)S(1)} %copy-done.6, ...), custom_call_target="tpu_custom_call" | custom-call | tf_op jit(solution)/shard_map/ffn_first_up/pallas_call | solution.py:351
  32.9 3.0 collective-permute-done.3.rest_1_
  37.7 12.0 %collective-permute-done.4.rest_1_ = bf16[4,128,512]{2,1,0:T(8,128)(2,1)} collective-permute-done((bf16[4,128,512]{2,1,0:T(8,128)(2,1)S(1)}, bf16[4,128,512]{2,1,0:T(8,128)(2,1)}, u32[]{:S(2)}, u32[]{:S(2)}) %collective-permute-start.4) | collective-permute-done | bytes 524320 | tf_op jit(solution)/shard_map/ppermute | solution.py:119
  54.1 2.7 ffn_first_down.1.x_ref
  56.8 12.2 %attend.1 = (f32[512,512]{1,0:T(8,128)S(1)}, bf16[512,512]{1,0:T(8,128)(2,1)S(1)}, bf16[3,4,512,128]{3,2,1,0:T(8,128)(2,1)S(1)}, bf16[16,256,256]{2,1,0:T(8,128)(2,1)S(1)}, bf16[512,512]{1,0:T(8,128)(2,1)S(1)}) custom-call(s32[3]{0:T(128)S(1)} %pad_add_fusion.place_ref, s32[2]{0:T(128)S(1)} %copy-done.25, f32[512,512]{1,0:T(8,128)S(1)} %ffn_first_down.1.x_ref, ...), custom_call_target="tpu_custom_call" | custom-call | tf_op jit(solution)/shard_map/attend/pallas_call | solution.py:351
  72.4 5.4 %convolve.1 = (f32[512,512]{1,0:T(8,128)S(1)}, bf16[512,512]{1,0:T(8,128)(2,1)S(1)}, f32[2,4,288,128]{3,2,1,0:T(8,128)S(1)}, f32[512,512]{1,0:T(8,128)S(1)}, f32...) custom-call(s32[3]{0:T(128)S(1)} %pad_add_fusion.place_ref, f32[512,512]{1,0:T(8,128)S(1)} %get-tuple-element.187.x_ref, ...), custom_call_target="tpu_custom_call" | custom-call | tf_op jit(solution)/shard_map/convolve/pallas_call | solution.py:351
  78.0 6.8 %collective-permute-done.11.rest_4_ = bf16[512,512]{1,0:T(8,128)(2,1)S(1)} collective-permute-done((bf16[512,512]{1,0:T(8,128)(2,1)S(1)}, bf16[512,512]{1,0:T(8,128)(2,1)S(1)}, u32[]{:S(2)}, u32[]{:S(2)}) %collective-permute-start.11) | collective-permute-done | bytes 524320 | tf_op jit(solution)/shard_map/ppermute | solution.py:119
  86.7 12.7 %ffn_last.1 = (bf16[512,512]{1,0:T(8,128)(2,1)}, f32[512,512]{1,0:T(8,128)S(1)}, f32[8,512]{1,0:T(8,128)S(1)}, bf16[16,128,512]{2,1,0:T(8,128)(2,1)S(1)}, bf16[16,128,512]{2,1,0:T(8,128)(2,1)S(1)}) custom-call(s32[3]{0:T(128)S(1)} %pad_add_fusion.place_ref, s32[2]{0:T(128)S(1)} %copy-done.25, f32[512,512]{1,0:T(8,128)S(1)} %get-tuple-element.192.x_ref, ...), custom_call_target="tpu_custom_call" | custom-call | tf_op jit(solution)/shard_map/ffn_last/pallas_call | solution.py:351
  99.6 15.3 %convolve_back.1 = (f32[512,512]{1,0:T(8,128)S(1)}, f32[8,512]{1,0:T(8,128)S(1)}, f32[32,512]{1,0:T(8,128)S(1)}, bf16[16,48,512]{2,1,0:T(8,128)(2,1)S(1)}, bf16[16,48,512]{2,1,0:T(8,128)(2,1)S(1)}) custom-call(s32[3]{0:T(128)S(1)} %pad_add_fusion.place_ref, f32[512,512]{1,0:T(8,128)S(1)} %get-tuple-element.204.grad_ref, ...), custom_call_target="tpu_custom_call" | custom-call | tf_op jit(solution)/shard_map/convolve_back/pallas_call | solution.py:351
  117.7 19.5 %attend_back.1 = (f32[512,512]{1,0:T(8,128)S(1)}, f32[8,512]{1,0:T(8,128)S(1)}, f32[512,128]{1,0:T(8,128)S(1)}, bf16[16,64,512]{2,1,0:T(8,128)(2,1)S(1)}, bf16[16,64,512]{2,1,0:T(8,128)(2,1)S(1)}) custom-call(s32[3]{0:T(128)S(1)} %pad_add_fusion.place_ref, f32[512,512]{1,0:T(8,128)S(1)} %get-tuple-element.215.grad_ref, f32[512,512]{1,0:T(8,128)S(1)} %ffn_first_down.1.x_ref, ...), custom_call_target="tpu_custom_call" | custom-call | tf_op jit(solution)/shard_map/attend_back/pallas_call | solution.py:351
  138.2 3.9 %collective-permute-done.14 = bf16[8,128,512]{2,1,0:T(8,128)(2,1)S(1)} collective-permute-done((bf16[8,128,512]{2,1,0:T(8,128)(2,1)S(1)}, bf16[8,128,512]{2,1,0:T(8,128)(2,1)S(1)}, u32[]{:S(2)}, u32[]{:S(2)}) %collective-permute-start.14) | collective-permute-done | bytes 1048608 | tf_op jit(solution)/shard_map/ppermute | solution.py:119
  144.0 4.5 %ffn_first_out.1 = (bf16[512,2048]{1,0:T(8,128)(2,1)S(1)}, bf16[16,64,512]{2,1,0:T(8,128)(2,1)S(1)}, bf16[16,64,512]{2,1,0:T(8,128)(2,1)S(1)}) custom-call(s32[3]{0:T(128)S(1)} %pad_add_fusion.place_ref, f32[512,512]{1,0:T(8,128)S(1)} %get-tuple-element.226.grad_ref, bf16[512,2048]{1,0:T(8,128)(2,1)S(1)} %get-tuple-element.182.hidden_ref, ...), custom_call_target="tpu_custom_call" | custom-call | tf_op jit(solution)/shard_map/ffn_first_out/pallas_call | solution.py:351
  150.8 4.2 %collective-permute-done.16 = bf16[4,128,512]{2,1,0:T(8,128)(2,1)S(1)} collective-permute-done((bf16[4,128,512]{2,1,0:T(8,128)(2,1)S(1)}, bf16[4,128,512]{2,1,0:T(8,128)(2,1)S(1)}, u32[]{:S(2)}, u32[]{:S(2)}) %collective-permute-start.16) | collective-permute-done | bytes 524320 | tf_op jit(solution)/shard_map/ppermute | solution.py:119
  156.7 6.1 %ffn_first_in.1 = (bf16[512,512]{1,0:T(8,128)(2,1)}, f32[8,512]{1,0:T(8,128)S(1)}, bf16[16,64,512]{2,1,0:T(8,128)(2,1)S(1)}, bf16[16,64,512]{2,1,0:T(8,128)(2,1)S(1)}) custom-call(s32[3]{0:T(128)S(1)} %pad_add_fusion.place_ref, f32[512,512]{1,0:T(8,128)S(1)} %get-tuple-element.226.grad_ref, bf16[512,512]{1,0:T(8,128)(2,1)S(1)} %bitcast.55, ...), custom_call_target="tpu_custom_call" | custom-call | tf_op jit(solution)/shard_map/ffn_first_in/pallas_call | solution.py:351
  165.3 2.6 collective-permute-start.23
  169.4 5.0 %collective-permute-done.23 = bf16[1,128,512]{2,1,0:T(8,128)(2,1)S(1)} collective-permute-done((bf16[1,128,512]{2,1,0:T(8,128)(2,1)S(1)}, bf16[1,128,512]{2,1,0:T(8,128)(2,1)S(1)}, u32[]{:S(2)}, u32[]{:S(2)}) %collective-permute-start.23) | collective-permute-done | bytes 131104 | tf_op jit(solution)/shard_map/ppermute | solution.py:119
  179.7 2.6 collective-permute-start.27
  188.6 7.3 %collective-permute-done.29 = bf16[8,64,512]{2,1,0:T(8,128)(2,1)S(1)} collective-permute-done((bf16[8,64,512]{2,1,0:T(8,128)(2,1)S(1)}, bf16[8,64,512]{2,1,0:T(8,128)(2,1)S(1)}, u32[]{:S(2)}, u32[]{:S(2)}) %collective-permute-start.29) | collective-permute-done | bytes 524320 | tf_op jit(solution)/shard_map/ppermute | solution.py:119
  199.0 13.1 %collective-permute-done.34 = f32[56,512]{1,0:T(8,128)S(1)} collective-permute-done((f32[56,512]{1,0:T(8,128)S(1)}, f32[56,512]{1,0:T(8,128)S(1)}, u32[]{:S(2)}, u32[]{:S(2)}) %collective-permute-start.34) | collective-permute-done | bytes 114720 | tf_op jit(solution)/shard_map/ppermute | solution.py:119
  215.7 4.9 %collective-permute-done.38 = f32[56,512]{1,0:T(8,128)S(1)} collective-permute-done((f32[56,512]{1,0:T(8,128)S(1)}, f32[56,512]{1,0:T(8,128)S(1)}, u32[]{:S(2)}, u32[]{:S(2)}) %collective-permute-start.38) | collective-permute-done | bytes 114720 | tf_op jit(solution)/shard_map/ppermute | solution.py:119
  226.8 2.7 collective-permute-start.47
  236.4 4.3 %collective-permute-done.40 = bf16[1,128,512]{2,1,0:T(8,128)(2,1)S(1)} collective-permute-done((bf16[1,128,512]{2,1,0:T(8,128)(2,1)S(1)}, bf16[1,128,512]{2,1,0:T(8,128)(2,1)S(1)}, u32[]{:S(2)}, u32[]{:S(2)}) %collective-permute-start.40) | collective-permute-done | bytes 131104 | tf_op jit(solution)/shard_map/ppermute | solution.py:119
  244.4 10.2 %update_out1.1 = (f32[2,1024,512]{2,1,0:T(8,128)}, f32[2,1024,512]{2,1,0:T(8,128)}, f32[2,1024,512]{2,1,0:T(8,128)}, f32[2,1024,512]{2,1,0:T(8,128)}, f32[8,128]{1,0:T(8,128)}) custom-call(s32[16]{0:T(128)} %broadcast_xor_fusion.spot_ref, bf16[8,128,512]{2,1,0:T(8,128)(2,1)} %copy-done.32, bf16[8,128,512]{2,1,0:T(8,128)(2,1)} %copy-done.34, ...), custom_call_target="tpu_custom_call" | custom-call | tf_op jit(solution)/shard_map/update_out1/pallas_call | solution.py:916
  257.0 10.3 %update_in1.1 = (f32[2,256,2048]{2,1,0:T(8,128)}, f32[2,256,2048]{2,1,0:T(8,128)}, f32[2,256,2048]{2,1,0:T(8,128)}, f32[2,256,2048]{2,1,0:T(8,128)}, f32[8,128]{1,0:T(8,128)}) custom-call(s32[16]{0:T(128)} %broadcast_xor_fusion.spot_ref, bf16[8,128,512]{2,1,0:T(8,128)(2,1)} %copy-done.32, bf16[8,128,512]{2,1,0:T(8,128)(2,1)} %copy-done.34, ...), custom_call_target="tpu_custom_call" | custom-call | tf_op jit(solution)/shard_map/update_in1/pallas_call | solution.py:916
  277.4 14.8 %update_rest.1 = (f32[4,256,512]{2,1,0:T(8,128)}, f32[4,256,512]{2,1,0:T(8,128)}, f32[4,256,512]{2,1,0:T(8,128)}, f32[3,256,512]{2,1,0:T(8,128)}, f32[256,512]{1...) custom-call(s32[16]{0:T(128)} %broadcast_xor_fusion.spot_ref, ...), custom_call_target="tpu_custom_call" | custom-call | tf_op jit(solution)/shard_map/update_rest/pallas_call | solution.py:1061
  297.6 5.7 %move_layer.2 = (f32[2,256,2048]{2,1,0:T(8,128)}, f32[2,1024,512]{2,1,0:T(8,128)}) custom-call(f32[2]{0:T(128)} %bitcast.57, f32[2,256,2048]{2,1,0:T(8,128)} %w0.4, f32[2,256,2048]{2,1,0:T(8,128)} %get-tuple-element.282.u0, f32[2,1024,512]{2,1,0:T(8,128)} %w1.4, f32[2,1024,512]{2,1,0:T(8,128)} %get-tuple-element.283.u1), custom_call_target="tpu_custom_call", output_to_operand_aliasing={{0}: (2, {}), {1}: (4, {})} | custom-call | tf_op jit(solution)/shard_map/move_layer/pallas_call | solution.py:944
  305.0 5.3 %move_rest.1 = (f32[4,256,512]{2,1,0:T(8,128)}, f32[256,1536]{1,0:T(8,128)}) custom-call(f32[6]{0:T(128)} %get-tuple-element.420.factor_ref, f32[4,256,512]{2,1,0:T(8,128)} %w0.5, f32[4,256,512]{2,1,0:T(8,128)} %get-tuple-element.306.u0, f32[256,1536]{1,0:T(8,128)} %w1.5, ...), custom_call_target="tpu_custom_call", output_to_operand_aliasing={{0}: (2, {}), {1}: (4, {})} | custom-call | tf_op jit(solution)/shard_map/move_rest/pallas_call | solution.py:968
  312.7 10.2 %update_out0.1 = (f32[2,1024,512]{2,1,0:T(8,128)}, f32[2,1024,512]{2,1,0:T(8,128)}, f32[2,1024,512]{2,1,0:T(8,128)}, f32[2,1024,512]{2,1,0:T(8,128)}, f32[8,128]{1,0:T(8,128)}) custom-call(s32[16]{0:T(128)} %broadcast_xor_fusion.spot_ref, bf16[8,128,512]{2,1,0:T(8,128)(2,1)} %copy-done.33, ...), custom_call_target="tpu_custom_call", output_to_operand_aliasing={{0}: (8, {}), {1}: (9, {}), {2}: (10, {}), {3}: (11, {})} | custom-call | tf_op jit(solution)/shard_map/update_out0/pallas_call | solution.py:916
  323.6 10.3 %update_in0.1 = (f32[2,256,2048]{2,1,0:T(8,128)}, f32[2,256,2048]{2,1,0:T(8,128)}, f32[2,256,2048]{2,1,0:T(8,128)}, f32[2,256,2048]{2,1,0:T(8,128)}, f32[8,128]{1,0:T(8,128)}) custom-call(s32[16]{0:T(128)} %broadcast_xor_fusion.spot_ref, bf16[8,128,512]{2,1,0:T(8,128)(2,1)} %copy-done.33, ...), custom_call_target="tpu_custom_call", output_to_operand_aliasing={{0}: (8, {}), {1}: (9, {}), {2}: (10, {}), {3}: (11, {})} | custom-call | tf_op jit(solution)/shard_map/update_in0/pallas_call | solution.py:916
  342.9 5.7 %move_layer.3 = (f32[2,256,2048]{2,1,0:T(8,128)}, f32[2,1024,512]{2,1,0:T(8,128)}) custom-call(f32[2]{0:T(128)} %get-tuple-element.414.factor_ref, f32[2,256,2048]{2,1,0:T(8,128)} %w0.4, f32[2,256,2048]{2,1,0:T(8,128)} %get-tuple-element.296.u0, f32[2,1024,512]{2,1,0:T(8,128)} %w1.4, ...), custom_call_target="tpu_custom_call", output_to_operand_aliasing={{0}: (2, {}), {1}: (4, {})} | custom-call | tf_op jit(solution)/shard_map/move_layer/pallas_call | solution.py:944
  (292 shorter events, 112.1 us)
Async XLA Ops:
  3.4 17.6 %collective-permute-start.1 = (bf16[128,2048]{1,0:T(8,128)(2,1)}, bf16[128,2048]{1,0:T(8,128)(2,1)}, u32[]{:S(2)}, u32[]{:S(2)}) collective-permute-start(bf16[128,2048]{1,0:T(8,128)(2,1)} %bitcast.66), channel_id=1, source_target_pairs={{0,1},{1,0},{2,3},{3,2},{4,5},{5,4},{6,7},{7,6},{8,9},{9,8},{10,11... | collective-permute-start | bytes 1572872 | tf_op jit(solution)/shard_map/ppermute | solution.py:119
  6.4 14.6 %collective-permute-start = (bf16[37,256]{1,0:T(8,128)(2,1)S(1)}, bf16[37,256]{1,0:T(8,128)(2,1)S(1)}, u32[]{:S(2)}, u32[]{:S(2)}) collective-permute-start(bf16[37,256]{1,0:T(8,128)(2,1)S(1)} %convert_element_type.322), channel_id=1, source_target_pairs={{0,1},{1,0},{2,3},{3,2},{4,5},{5,4},{6,7},{7,6},{8,9},{9,8},{10,11... | collective-permute-start | bytes 56840 | tf_op jit(solution)/shard_map/ppermute | solution.py:119
  21.1 14.9 %collective-permute-start.3 = (bf16[512,512]{1,0:T(8,128)(2,1)}, bf16[512,512]{1,0:T(8,128)(2,1)}, u32[]{:S(2)}, u32[]{:S(2)}) collective-permute-start(bf16[512,512]{1,0:T(8,128)(2,1)} %bitcast.65), channel_id=1, source_target_pairs={{0,1},{1,0},{2,3},{3,2},{4,5},{5,4},{6,7},{7,6},{8,9},{9,8},{10,11... | collective-permute-start | bytes 1572872 | tf_op jit(solution)/shard_map/ppermute | solution.py:119
  35.9 13.7 %collective-permute-start.4 = (bf16[4,128,512]{2,1,0:T(8,128)(2,1)S(1)}, bf16[4,128,512]{2,1,0:T(8,128)(2,1)}, u32[]{:S(2)}, u32[]{:S(2)}) collective-permute-start(bf16[4,128,512]{2,1,0:T(8,128)(2,1)S(1)} %copy-done.30), channel_id=1, source_target_pairs={{0,1},{1,0},{2,3},{3,2},{4,5},{5,4},{6,7},{7,6},{8,9},{9,8},{10,11... | collective-permute-start | bytes 1572872 | tf_op jit(solution)/shard_map/ppermute | solution.py:119
  37.7 15.2 %collective-permute-start.5 = (bf16[512,512]{1,0:T(8,128)(2,1)}, bf16[512,512]{1,0:T(8,128)(2,1)}, u32[]{:S(2)}, u32[]{:S(2)}) collective-permute-start(bf16[512,512]{1,0:T(8,128)(2,1)} %collective-permute-done.3.rest_1_), channel_id=1, source_target_pairs={{0,2},{2,0},{4,6},{6,4},{8,10},{10,8},{12,14},{14,12},{16,18},{18,... | collective-permute-start | bytes 1572872 | tf_op jit(solution)/shard_map/ppermute | solution.py:119
  50.5 20.1 %collective-permute-start.7 = (bf16[128,1536]{1,0:T(8,128)(2,1)}, bf16[128,1536]{1,0:T(8,128)(2,1)S(1)}, u32[]{:S(2)}, u32[]{:S(2)}) collective-permute-start(bf16[128,1536]{1,0:T(8,128)(2,1)} %copy-done.31), channel_id=1, source_target_pairs={{0,1},{1,0},{2,3},{3,2},{4,5},{5,4},{6,7},{7,6},{8,9},{9,8},{10,11... | collective-permute-start | bytes 1179656 | tf_op jit(solution)/shard_map/ppermute | solution.py:119
  52.3 25.5 %collective-permute-start.9 = (bf16[128,2048]{1,0:T(8,128)(2,1)}, bf16[128,2048]{1,0:T(8,128)(2,1)S(1)}, u32[]{:S(2)}, u32[]{:S(2)}) collective-permute-start(bf16[128,2048]{1,0:T(8,128)(2,1)} %copy-done.28), channel_id=1, source_target_pairs={{0,1},{1,0},{2,3},{3,2},{4,5},{5,4},{6,7},{7,6},{8,9},{9,8},{10,11... | collective-permute-start | bytes 1572872 | tf_op jit(solution)/shard_map/ppermute | solution.py:119
  69.0 15.8 %collective-permute-start.11 = (bf16[512,512]{1,0:T(8,128)(2,1)S(1)}, bf16[512,512]{1,0:T(8,128)(2,1)S(1)}, u32[]{:S(2)}, u32[]{:S(2)}) collective-permute-start(bf16[512,512]{1,0:T(8,128)(2,1)S(1)} %copy-done.27), channel_id=1, source_target_pairs={{0,1},{1,0},{2,3},{3,2},{4,5},{5,4},{6,7},{7,6},{8,9},{9,8},{10,11... | collective-permute-start | bytes 1572872 | tf_op jit(solution)/shard_map/ppermute | solution.py:119
  99.4 16.0 %collective-permute-start.13 = (bf16[16,128,512]{2,1,0:T(8,128)(2,1)S(1)}, bf16[16,128,512]{2,1,0:T(8,128)(2,1)S(1)}, u32[]{:S(2)}, u32[]{:S(2)}) collective-permute-start(bf16[16,128,512]{2,1,0:T(8,128)(2,1)S(1)} %get-tuple-element.203), channel_id=1, source_target_pairs={{0,2},{2,0},{4,6},{6,4},{8,10},{10,8},{12,14},{14,12},{16,18},{18,... | collective-permute-start | bytes 6291464 | tf_op jit(solution)/shard_map/ppermute | solution.py:119
  114.9 22.4 %collective-permute-start.15 = (bf16[16,48,512]{2,1,0:T(8,128)(2,1)S(1)}, bf16[16,48,512]{2,1,0:T(8,128)(2,1)S(1)}, u32[]{:S(2)}, u32[]{:S(2)}) collective-permute-start(bf16[16,48,512]{2,1,0:T(8,128)(2,1)S(1)} %get-tuple-element.214), channel_id=1, source_target_pairs={{0,2},{2,0},{4,6},{6,4},{8,10},{10,8},{12,14},{14,12},{16,18},{18,... | collective-permute-start | bytes 2359304 | tf_op jit(solution)/shard_map/ppermute | solution.py:119
  116.1 25.9 %collective-permute-start.14 = (bf16[8,128,512]{2,1,0:T(8,128)(2,1)S(1)}, bf16[8,128,512]{2,1,0:T(8,128)(2,1)S(1)}, u32[]{:S(2)}, u32[]{:S(2)}) collective-permute-start(bf16[8,128,512]{2,1,0:T(8,128)(2,1)S(1)} %get-tuple-element.381), channel_id=1, source_target_pairs={{0,1},{1,0},{2,3},{3,2},{4,5},{5,4},{6,7},{7,6},{8,9},{9,8},{10,11... | collective-permute-start | bytes 3145736 | tf_op jit(solution)/shard_map/ppermute | solution.py:119
  137.6 13.0 %collective-permute-start.18 = (bf16[8,48,512]{2,1,0:T(8,128)(2,1)S(1)}, bf16[8,48,512]{2,1,0:T(8,128)(2,1)S(1)}, u32[]{:S(2)}, u32[]{:S(2)}) collective-permute-start(bf16[8,48,512]{2,1,0:T(8,128)(2,1)S(1)} %get-tuple-element.391), channel_id=1, source_target_pairs={{0,1},{1,0},{2,3},{3,2},{4,5},{5,4},{6,7},{7,6},{8,9},{9,8},{10,11... | collective-permute-start | bytes 1179656 | tf_op jit(solution)/shard_map/ppermute | solution.py:119
  142.4 12.5 %collective-permute-start.16 = (bf16[4,128,512]{2,1,0:T(8,128)(2,1)S(1)}, bf16[4,128,512]{2,1,0:T(8,128)(2,1)S(1)}, u32[]{:S(2)}, u32[]{:S(2)}) collective-permute-start(bf16[4,128,512]{2,1,0:T(8,128)(2,1)S(1)} %get-tuple-element.389), channel_id=1, source_target_pairs={{0,4},{2,6},{4,0},{6,2},{8,12},{10,14},{12,8},{14,10},{16,20},{18,... | collective-permute-start | bytes 1572872 | tf_op jit(solution)/shard_map/ppermute | solution.py:119
  148.9 14.1 %collective-permute-start.19 = (bf16[8,64,512]{2,1,0:T(8,128)(2,1)S(1)}, bf16[8,64,512]{2,1,0:T(8,128)(2,1)S(1)}, u32[]{:S(2)}, u32[]{:S(2)}) collective-permute-start(bf16[8,64,512]{2,1,0:T(8,128)(2,1)S(1)} %get-tuple-element.387), channel_id=1, source_target_pairs={{0,1},{1,0},{2,3},{3,2},{4,5},{5,4},{6,7},{7,6},{8,9},{9,8},{10,11... | collective-permute-start | bytes 1572872 | tf_op jit(solution)/shard_map/ppermute | solution.py:119
  150.6 12.7 %collective-permute-start.21 = (bf16[16,64,512]{2,1,0:T(8,128)(2,1)S(1)}, bf16[16,64,512]{2,1,0:T(8,128)(2,1)S(1)}, u32[]{:S(2)}, u32[]{:S(2)}) collective-permute-start(bf16[16,64,512]{2,1,0:T(8,128)(2,1)S(1)} %get-tuple-element.232), channel_id=1, source_target_pairs={{0,2},{2,0},{4,6},{6,4},{8,10},{10,8},{12,14},{14,12},{16,18},{18,... | collective-permute-start | bytes 3145736 | tf_op jit(solution)/shard_map/ppermute | solution.py:119
  163.7 13.1 %collective-permute-start.24 = (bf16[16,64,512]{2,1,0:T(8,128)(2,1)S(1)}, bf16[16,64,512]{2,1,0:T(8,128)(2,1)S(1)}, u32[]{:S(2)}, u32[]{:S(2)}) collective-permute-start(bf16[16,64,512]{2,1,0:T(8,128)(2,1)S(1)} %get-tuple-element.248), channel_id=1, source_target_pairs={{0,2},{2,0},{4,6},{6,4},{8,10},{10,8},{12,14},{14,12},{16,18},{18,... | collective-permute-start | bytes 3145736 | tf_op jit(solution)/shard_map/ppermute | solution.py:119
  163.7 12.9 %collective-permute-start.22 = (bf16[4,112,512]{2,1,0:T(8,128)(2,1)S(1)}, bf16[4,112,512]{2,1,0:T(8,128)(2,1)S(1)}, u32[]{:S(2)}, u32[]{:S(2)}) collective-permute-start(bf16[4,112,512]{2,1,0:T(8,128)(2,1)S(1)} %pad_maximum_fusion.3), channel_id=1, source_target_pairs={{0,4},{2,6},{4,0},{6,2},{8,12},{10,14},{12,8},{14,10},{16,20},{18,... | collective-permute-start | bytes 1376264 | tf_op jit(solution)/shard_map/ppermute | solution.py:119
  167.9 14.8 %collective-permute-start.28 = (bf16[8,64,512]{2,1,0:T(8,128)(2,1)S(1)}, bf16[8,64,512]{2,1,0:T(8,128)(2,1)S(1)}, u32[]{:S(2)}, u32[]{:S(2)}) collective-permute-start(bf16[8,64,512]{2,1,0:T(8,128)(2,1)S(1)} %get-tuple-element.252), channel_id=1, source_target_pairs={{0,1},{1,0},{2,3},{3,2},{4,5},{5,4},{6,7},{7,6},{8,9},{9,8},{10,11... | collective-permute-start | bytes 1572872 | tf_op jit(solution)/shard_map/ppermute | solution.py:119
  178.7 17.2 %collective-permute-start.29 = (bf16[8,64,512]{2,1,0:T(8,128)(2,1)S(1)}, bf16[8,64,512]{2,1,0:T(8,128)(2,1)S(1)}, u32[]{:S(2)}, u32[]{:S(2)}) collective-permute-start(bf16[8,64,512]{2,1,0:T(8,128)(2,1)S(1)} %get-tuple-element.253), channel_id=1, source_target_pairs={{0,1},{1,0},{2,3},{3,2},{4,5},{5,4},{6,7},{7,6},{8,9},{9,8},{10,11... | collective-permute-start | bytes 1572872 | tf_op jit(solution)/shard_map/ppermute | solution.py:119
  196.1 16.2 %collective-permute-start.33 = (bf16[4,128,512]{2,1,0:T(8,128)(2,1)S(1)}, bf16[4,128,512]{2,1,0:T(8,128)(2,1)S(1)}, u32[]{:S(2)}, u32[]{:S(2)}) collective-permute-start(bf16[4,128,512]{2,1,0:T(8,128)(2,1)S(1)} %pad_maximum_fusion.1), channel_id=1, source_target_pairs={{0,4},{2,6},{4,0},{6,2},{8,12},{10,14},{12,8},{14,10},{16,20},{18,... | collective-permute-start | bytes 1572872 | tf_op jit(solution)/shard_map/ppermute | solution.py:119
  196.7 15.4 %collective-permute-start.34 = (f32[56,512]{1,0:T(8,128)S(1)}, f32[56,512]{1,0:T(8,128)S(1)}, u32[]{:S(2)}, u32[]{:S(2)}) collective-permute-start(f32[56,512]{1,0:T(8,128)S(1)} %add.245), channel_id=1, source_target_pairs={{0,4},{2,6},{4,0},{6,2},{8,12},{10,14},{12,8},{14,10},{16,20},{18,... | collective-permute-start | bytes 344072 | tf_op jit(solution)/shard_map/ppermute | solution.py:119
  198.2 13.9 %collective-permute-start.31 = (bf16[1,112,512]{2,1,0:T(8,128)(2,1)S(1)}, bf16[1,112,512]{2,1,0:T(8,128)(2,1)S(1)}, u32[]{:S(2)}, u32[]{:S(2)}) collective-permute-start(bf16[1,112,512]{2,1,0:T(8,128)(2,1)S(1)} %add_convert_fusion.33), channel_id=1, source_target_pairs={{0,16},{2,18},{4,20},{6,22},{8,24},{10,26},{12,28},{14,30},{16,0},... | collective-permute-start | bytes 344072 | tf_op jit(solution)/shard_map/ppermute | solution.py:119
  198.6 13.7 %collective-permute-start.32 = (bf16[2,128,512]{2,1,0:T(8,128)(2,1)S(1)}, bf16[2,128,512]{2,1,0:T(8,128)(2,1)S(1)}, u32[]{:S(2)}, u32[]{:S(2)}) collective-permute-start(bf16[2,128,512]{2,1,0:T(8,128)(2,1)S(1)} %pad_maximum_fusion.6), channel_id=1, source_target_pairs={{0,8},{2,10},{4,12},{6,14},{8,0},{10,2},{12,4},{14,6},{16,24},{18,... | collective-permute-start | bytes 786440 | tf_op jit(solution)/shard_map/ppermute | solution.py:119
  213.0 11.5 %collective-permute-start.37 = (bf16[2,128,512]{2,1,0:T(8,128)(2,1)S(1)}, bf16[2,128,512]{2,1,0:T(8,128)(2,1)S(1)}, u32[]{:S(2)}, u32[]{:S(2)}) collective-permute-start(bf16[2,128,512]{2,1,0:T(8,128)(2,1)S(1)} %get-tuple-element.261), channel_id=1, source_target_pairs={{0,8},{2,10},{4,12},{6,14},{8,0},{10,2},{12,4},{14,6},{16,24},{18,... | collective-permute-start | bytes 786440 | tf_op jit(solution)/shard_map/ppermute | solution.py:119
  214.6 12.0 %collective-permute-start.36 = (bf16[4,128,512]{2,1,0:T(8,128)(2,1)S(1)}, bf16[4,128,512]{2,1,0:T(8,128)(2,1)S(1)}, u32[]{:S(2)}, u32[]{:S(2)}) collective-permute-start(bf16[4,128,512]{2,1,0:T(8,128)(2,1)S(1)} %pad_maximum_fusion.2), channel_id=1, source_target_pairs={{0,4},{2,6},{4,0},{6,2},{8,12},{10,14},{12,8},{14,10},{16,20},{18,... | collective-permute-start | bytes 1572872 | tf_op jit(solution)/shard_map/ppermute | solution.py:119
  231.0 12.4 %collective-permute-start.41 = (bf16[8,128,512]{2,1,0:T(8,128)(2,1)S(1)}, bf16[8,128,512]{2,1,0:T(8,128)(2,1)S(1)}, u32[]{:S(2)}, u32[]{:S(2)}) collective-permute-start(bf16[8,128,512]{2,1,0:T(8,128)(2,1)S(1)} %pad_maximum_fusion.g0_near.g1_near), channel_id=1, source_target_pairs={{0,2},{2,0},{4,6},{6,4},{8,10},{10,8},{12,14},{14,12},{16,18},{18,... | collective-permute-start | bytes 3145736 | tf_op jit(solution)/shard_map/ppermute | solution.py:119
  240.8 13.9 %collective-permute-start.43 = (bf16[1,128,512]{2,1,0:T(8,128)(2,1)S(1)}, bf16[1,128,512]{2,1,0:T(8,128)(2,1)S(1)}, u32[]{:S(2)}, u32[]{:S(2)}) collective-permute-start(bf16[1,128,512]{2,1,0:T(8,128)(2,1)S(1)} %add_convert_fusion.26), channel_id=1, source_target_pairs={{0,16},{2,18},{4,20},{6,22},{8,24},{10,26},{12,28},{14,30},{16,0},... | collective-permute-start | bytes 393224 | tf_op jit(solution)/shard_map/ppermute | solution.py:119
  242.2 13.1 %collective-permute-start.42 = (bf16[4,112,512]{2,1,0:T(8,128)(2,1)S(1)}, bf16[4,112,512]{2,1,0:T(8,128)(2,1)S(1)}, u32[]{:S(2)}, u32[]{:S(2)}) collective-permute-start(bf16[4,112,512]{2,1,0:T(8,128)(2,1)S(1)} %pad_maximum_fusion.4), channel_id=1, source_target_pairs={{0,4},{2,6},{4,0},{6,2},{8,12},{10,14},{12,8},{14,10},{16,20},{18,... | collective-permute-start | bytes 1376264 | tf_op jit(solution)/shard_map/ppermute | solution.py:119
  254.6 12.7 %collective-permute-start.44 = (bf16[2,128,512]{2,1,0:T(8,128)(2,1)S(1)}, bf16[2,128,512]{2,1,0:T(8,128)(2,1)}, u32[]{:S(2)}, u32[]{:S(2)}) collective-permute-start(bf16[2,128,512]{2,1,0:T(8,128)(2,1)S(1)} %constant_dynamic-update-slice_fusion.2), channel_id=1, source_target_pairs={{0,8},{2,10},{4,12},{6,14},{8,0},{10,2},{12,4},{14,6},{16,24},{18,... | collective-permute-start | bytes 786440 | tf_op jit(solution)/shard_map/ppermute | solution.py:119
  255.4 21.1 %collective-permute-start.45 = (bf16[8,112,512]{2,1,0:T(8,128)(2,1)S(1)}, bf16[8,112,512]{2,1,0:T(8,128)(2,1)S(1)}, u32[]{:S(2)}, u32[]{:S(2)}) collective-permute-start(bf16[8,112,512]{2,1,0:T(8,128)(2,1)S(1)} %constant_dynamic-update-slice_fusion.g0_near.g1_near), channel_id=1, source_target_pairs={{0,2},{2,0},{4,6},{6,4},{8,10},{10,8},{12,14},{14,12},{16,18},{18,... | collective-permute-start | bytes 2752520 | tf_op jit(solution)/shard_map/ppermute | solution.py:119
  268.4 23.9 %collective-permute-start.46 = (bf16[4,128,512]{2,1,0:T(8,128)(2,1)S(1)}, bf16[4,128,512]{2,1,0:T(8,128)(2,1)S(1)}, u32[]{:S(2)}, u32[]{:S(2)}) collective-permute-start(bf16[4,128,512]{2,1,0:T(8,128)(2,1)S(1)} %constant_dynamic-update-slice_fusion.4), channel_id=1, source_target_pairs={{0,4},{2,6},{4,0},{6,2},{8,12},{10,14},{12,8},{14,10},{16,20},{18,... | collective-permute-start | bytes 1572872 | tf_op jit(solution)/shard_map/ppermute | solution.py:119
  292.3 19.4 %collective-permute-start.49 = (bf16[8,128,512]{2,1,0:T(8,128)(2,1)S(1)}, bf16[8,128,512]{2,1,0:T(8,128)(2,1)S(1)}, u32[]{:S(2)}, u32[]{:S(2)}) collective-permute-start(bf16[8,128,512]{2,1,0:T(8,128)(2,1)S(1)} %constant_dynamic-update-slice_fusion.6.g0_near.g1_near), channel_id=1, source_target_pairs={{0,2},{2,0},{4,6},{6,4},{8,10},{10,8},{12,14},{14,12},{16,18},{18,... | collective-permute-start | bytes 3145736 | tf_op jit(solution)/shard_map/ppermute | solution.py:119
  (68 other events, 458.9 us)

commit v2 on v1

--- a/solution.py
+++ b/solution.py
@@ -378,22 +378,18 @@
     return sum_ref[...]
 
 
-def ffn_behind(grad, values, gain, win, wout, entry_ref, hidden_ref, slope_ref, sum_ref, out_refs, plan, place_ref):
+def ffn_behind(grad, values, gain, win, wout, entry_ref, hidden_ref, slope_ref, out_refs, plan, place_ref):
     normed, scale = stats(values)
+    entry = entry_ref[...]
     branch = (0.5 * grad).astype(bf16)
-    sum_ref[...] = jnp.zeros_like(sum_ref)
-
-    def step(b, carry):
-        cols = pl.ds(pl.multiple_of(b * D, D), D)
-        shift = jnp.bitwise_xor((b % 2) * plan.place(8), (b // 2) * plan.place(16))
-        put(out_refs, plan, place_ref, dot_rows(hidden_ref[:, cols], branch), 64, 64, 0, shift)
+    grad_entry = jnp.zeros(values.shape, f32)
+    for b in range(FF // D):
+        cols = slice(b * D, (b + 1) * D)
+        put(out_refs, plan, place_ref, dot_rows(hidden_ref[:, cols], branch), 64, 64, 8 * b)
         grad_before = (dot_cols(branch, wout[cols, :]) * slope_ref[:, cols].astype(f32)).astype(bf16)
-        put(out_refs, plan, place_ref, dot_rows(entry_ref[...], grad_before), pl.multiple_of(16 * b, 16), 16, 0)
-        sum_ref[...] += dot_cols(grad_before, win[:, cols])
-        return carry
-
-    lax.fori_loop(0, FF // D, step, 0)
-    back, grad_gain = norm_back(sum_ref[...], normed, scale, gain)
+        put(out_refs, plan, place_ref, dot_rows(entry, grad_before), 16 * b, 16, 0)
+        grad_entry = grad_entry + dot_cols(grad_before, win[:, cols])
+    back, grad_gain = norm_back(grad_entry, normed, scale, gain)
     return grad + back, grad_gain
 
 
@@ -457,12 +453,12 @@
     def kernel(place_ref, len_ref, x_ref, vec_ref, cot_ref, *rest):
         wins, wouts = rest[:n], rest[n : 2 * n]
         y_ref, dx_ref, gain_ref, *g_refs = rest[2 * n : 2 * n + 5]
-        win, wout, entry_ref, hidden_ref, slope_ref, sum_ref = rest[2 * n + 5 :]
+        win, wout, entry_ref, hidden_ref, slope_ref = rest[2 * n + 5 :]
         join(place_ref, wins, win)
         join(place_ref, wouts, wout)
         x = x_ref[...]
         gain = vec_ref[35:36, :]
-        total = ffn_ahead(x, gain, win, wout, entry_ref, hidden_ref, slope_ref, sum_ref)
+        total = ffn_ahead(x, gain, win, wout, entry_ref, hidden_ref, slope_ref, dx_ref)
         normed, scale = stats(x + 0.5 * total)
         top = vec_ref[36:37, :]
         y_ref[...] = (normed * top).astype(bf16)
@@ -474,7 +470,7 @@
             grads.append(jnp.where(spot < len_ref[s], part, 0.0))
         back, grad_top = norm_back(jnp.concatenate(grads, axis=0), normed, scale, top)
         grad, grad_gain = ffn_behind(
-            back, x, gain, win, wout, entry_ref, hidden_ref, slope_ref, sum_ref, g_refs, plan, place_ref
+            back, x, gain, win, wout, entry_ref, hidden_ref, slope_ref, g_refs, plan, place_ref
         )
         dx_ref[...] = grad
         gain_ref[...] = jnp.concatenate([grad_gain, grad_top, jnp.zeros((6, D), f32)], axis=0)
@@ -490,7 +486,6 @@
             pltpu.VMEM((rows, D), bf16),
             pltpu.VMEM((rows, FF), bf16),
             pltpu.VMEM((rows, FF), bf16),
-            pltpu.VMEM((rows, D), f32),
         ],
         "ffn_last",
     )
@@ -577,10 +572,14 @@
         normed, _ = stats(x)
         entry = (normed * vec_ref[32:33, :]).astype(bf16)
         entry_ref[...] = entry
-        for k in range(3):
-            heads = dot(entry, weight[k]).astype(bf16)
+
+        def project(k, carry):
+            heads = dot(entry_ref[...], weight[k]).astype(bf16)
             for p in range(pairs):
                 qkv_ref[k, p] = heads[:, p * 128 : (p + 1) * 128]
+            return carry
+
+        lax.fori_loop(0, 3, project, 0)
         lane = lax.broadcasted_iota(jnp.int32, (1, 128), 1)
         table = rel_ref[...]
         spot = lax.broadcasted_iota(jnp.int32, (1, each), 1)
@@ -696,12 +695,17 @@
             return carry
 
         lax.fori_loop(0, count * pairs, step, 0)
-        entry_low = entry_ref[...]
-        grad_entry = jnp.zeros((rows, D), f32)
-        for k in range(3):
+        dx_ref[...] = jnp.zeros_like(dx_ref)
+
+        def project_back(k, carry):
             heads = jnp.concatenate([dqkv[k, p] for p in range(pairs)], axis=1)
-            put(g_refs, plan, place_ref, dot_rows(entry_low, heads), 16 * k, 16, 0)
-            grad_entry = grad_entry + dot_cols(heads, weight[k])
+            row = pl.multiple_of(16 * k, 16)
+            put(g_refs, plan, place_ref, dot_rows(entry_ref[...], heads), row, 16, 0)
+            dx_ref[...] += dot_cols(heads, weight[k])
+            return carry
+
+        lax.fori_loop(0, 3, project_back, 0)
+        grad_entry = dx_ref[...]
         normed, scale = stats(x_ref[...])
         back, grad_gain = norm_back(grad_entry, normed, scale, vec_ref[32:33, :])
         dx_ref[...] = down + back
@@ -749,8 +753,9 @@
             for c in range(cols):
                 gated_ref[s, c, :LEAD, :] = jnp.zeros((LEAD, 128), f32)
                 gated_ref[s, c, LEAD:, :] = gated[s * each : (s + 1) * each, c * 128 : (c + 1) * 128]
-        for c in range(cols):
-            taps = vec_ref[0:32, c * 128 : (c + 1) * 128]
+        def column(c, outer):
+            lanes = pl.ds(pl.multiple_of(c * 128, 128), 128)
+            taps = vec_ref[0:32, lanes]
 
             def step(i, carry):
                 s = i // (each // chunk)
@@ -758,10 +763,13 @@
                 total = jnp.zeros((chunk, 128), f32)
                 for k in range(KERNEL):
                     total = total + taps[k : k + 1] * gated_ref[s, c, pl.ds(t + k + LEAD - KERNEL + 1, chunk), :]
-                conv_ref[pl.ds(pl.multiple_of(i * chunk, chunk), chunk), c * 128 : (c + 1) * 128] = total
+                conv_ref[pl.ds(pl.multiple_of(i * chunk, chunk), chunk), lanes] = total
                 return carry
 
             lax.fori_loop(0, rows // chunk, step, 0)
+            return outer
+
+        lax.fori_loop(0, cols, column, 0)
         inner, _ = stats(conv_ref[...])
         act = inner * vec_ref[34:35, :]
         low = (act * logistic(act)).astype(bf16)
@@ -809,8 +817,8 @@
             for c in range(cols):
                 dconv[s, c, :each, :] = grad_conv[s * each : (s + 1) * each, c * 128 : (c + 1) * 128]
                 dconv[s, c, each:, :] = jnp.zeros((LEAD, 128), f32)
-        for c in range(cols):
-            lanes = slice(c * 128, (c + 1) * 128)
+        def column(c, outer):
+            lanes = pl.ds(pl.multiple_of(c * 128, 128), 128)
             taps = vec_ref[0:32, lanes]
 
             def step(i, sums):
@@ -828,6 +836,9 @@
             sums = lax.fori_loop(0, rows // 8, step, tuple(jnp.zeros((8, 128), f32) for _ in range(KERNEL)))
             found = [jnp.sum(v, axis=0, keepdims=True) for v in sums]
             taps_out[:, lanes] = jnp.concatenate(found + [jnp.zeros((1, 128), f32)], axis=0)
+            return outer
+
+        lax.fori_loop(0, cols, column, 0)
         grad_gated = dgated[...]
         sig_wide = sig_ref[...]
         linear_sig = jnp.concatenate(

time: 351 us -> 350 us (level)
  transfers between devices with their start and end apart: 51 -> 51, of which waited for: 24 -> 25; matrix products, arithmetic and copies ran while one was open for 6% -> 6% of each run, Pallas kernels for 34% -> 34%
where the time goes in v2:
time: 350 us; the launch traced here: 348 us
  Pallas kernels  160 us (46%)
  waiting for transfers between devices  87.3 us (25%)
  starting transfers between devices  45.1 us (13%)
  local copies, waits for them, and re-layouts  35.7 us (10%)
  other arithmetic  16.9 us (5%)
  between operations  3.62 us (1%)
    ppermute x51, waiting for transfers between devices, swap(): return lax.ppermute(values, axis, [(i, i ^ 1 << bit) for i in range(count)])  87.3 us
    pallas_call x11, Pallas kernels, call(): pl.pallas_call(kernel, out_shape=list(outs), in_specs=specs, out_specs=[v...  84.6 us
    ppermute x51, starting transfers between devices, swap(): return lax.ppermute(values, axis, [(i, i ^ 1 << bit) for i in range(count)])  45.1 us
    pallas_call x4, Pallas kernels, update_matrix(): pl.pallas_call(kernel, out_shape=[shape(states[0].shape, f32)] * 4 + [sha...  41 us
    unnamed x113, local copies, waits for them, and re-layouts  27.6 us
    pallas_call x1, Pallas kernels, update_rest(): pl.pallas_call(kernel, out_shape=[shape(attn[0].shape, f32)] * 3 + [shape...  14.8 us
    pallas_call x2, Pallas kernels, move_layer(): pl.pallas_call(kernel, out_shape=[shape(win.shape, f32), shape(wout.shape...  11.4 us
  transfers between devices with their start and end apart: 51, of which 25 were waited for; matrix products, arithmetic and copies ran while one was open for 6% of the time, Pallas kernels for 34%

profile of v2, /device:TPU:0, one launch (start us, length us, event | category | flops | bytes accessed | tf_op | source)
XLA Modules:
  0.0 348.5 jit_solution(3148990793843089719)
XLA Ops:
  0.7 2.7 rounded_halves.1
  3.4 3.0 collective-permute-start.1
  26.2 4.5 %ffn_first_up.1 = (bf16[512,512]{1,0:T(8,128)(2,1)S(1)}, bf16[512,2048]{1,0:T(8,128)(2,1)S(1)}, bf16[512,2048]{1,0:T(8,128)(2,1)S(1)}) custom-call(s32[3]{0:T(128)S(1)} %pad_add_fusion.place_ref, bf16[512,512]{1,0:T(8,128)(2,1)S(1)} %bitcast.53, f32[40,512]{1,0:T(8,128)S(1)} %pad_convert_fusion.vec_ref, bf16[256,2048]{1,0:T(8,128)(2,1)S(1)} %copy-done.6, ...), custom_call_target="tpu_custom_call" | custom-call | tf_op jit(solution)/shard_map/ffn_first_up/pallas_call | solution.py:351
  32.9 3.0 collective-permute-done.3.rest_1_
  37.7 12.0 %collective-permute-done.4.rest_1_ = bf16[4,128,512]{2,1,0:T(8,128)(2,1)} collective-permute-done((bf16[4,128,512]{2,1,0:T(8,128)(2,1)S(1)}, bf16[4,128,512]{2,1,0:T(8,128)(2,1)}, u32[]{:S(2)}, u32[]{:S(2)}) %collective-permute-start.4) | collective-permute-done | bytes 524320 | tf_op jit(solution)/shard_map/ppermute | solution.py:119
  54.1 2.7 ffn_first_down.1.x_ref
  56.8 12.6 %attend.1 = (f32[512,512]{1,0:T(8,128)S(1)}, bf16[512,512]{1,0:T(8,128)(2,1)S(1)}, bf16[3,4,512,128]{3,2,1,0:T(8,128)(2,1)S(1)}, bf16[16,256,256]{2,1,0:T(8,128)(2,1)S(1)}, bf16[512,512]{1,0:T(8,128)(2,1)S(1)}) custom-call(s32[3]{0:T(128)S(1)} %pad_add_fusion.place_ref, s32[2]{0:T(128)S(1)} %copy-done.25, f32[512,512]{1,0:T(8,128)S(1)} %ffn_first_down.1.x_ref, ...), custom_call_target="tpu_custom_call" | custom-call | tf_op jit(solution)/shard_map/attend/pallas_call | solution.py:351
  72.7 5.4 %convolve.1 = (f32[512,512]{1,0:T(8,128)S(1)}, bf16[512,512]{1,0:T(8,128)(2,1)S(1)}, f32[2,4,288,128]{3,2,1,0:T(8,128)S(1)}, f32[512,512]{1,0:T(8,128)S(1)}, f32...) custom-call(s32[3]{0:T(128)S(1)} %pad_add_fusion.place_ref, f32[512,512]{1,0:T(8,128)S(1)} %get-tuple-element.187.x_ref, ...), custom_call_target="tpu_custom_call" | custom-call | tf_op jit(solution)/shard_map/convolve/pallas_call | solution.py:351
  78.4 6.4 %collective-permute-done.11.rest_4_ = bf16[512,512]{1,0:T(8,128)(2,1)S(1)} collective-permute-done((bf16[512,512]{1,0:T(8,128)(2,1)S(1)}, bf16[512,512]{1,0:T(8,128)(2,1)S(1)}, u32[]{:S(2)}, u32[]{:S(2)}) %collective-permute-start.11) | collective-permute-done | bytes 524320 | tf_op jit(solution)/shard_map/ppermute | solution.py:119
  86.7 12.3 %ffn_last.1 = (bf16[512,512]{1,0:T(8,128)(2,1)}, f32[512,512]{1,0:T(8,128)S(1)}, f32[8,512]{1,0:T(8,128)S(1)}, bf16[16,128,512]{2,1,0:T(8,128)(2,1)S(1)}, bf16[16,128,512]{2,1,0:T(8,128)(2,1)S(1)}) custom-call(s32[3]{0:T(128)S(1)} %pad_add_fusion.place_ref, s32[2]{0:T(128)S(1)} %copy-done.25, f32[512,512]{1,0:T(8,128)S(1)} %get-tuple-element.192.x_ref, ...), custom_call_target="tpu_custom_call" | custom-call | tf_op jit(solution)/shard_map/ffn_last/pallas_call | solution.py:351
  99.2 15.2 %convolve_back.1 = (f32[512,512]{1,0:T(8,128)S(1)}, f32[8,512]{1,0:T(8,128)S(1)}, f32[32,512]{1,0:T(8,128)S(1)}, bf16[16,48,512]{2,1,0:T(8,128)(2,1)S(1)}, bf16[16,48,512]{2,1,0:T(8,128)(2,1)S(1)}) custom-call(s32[3]{0:T(128)S(1)} %pad_add_fusion.place_ref, f32[512,512]{1,0:T(8,128)S(1)} %get-tuple-element.204.grad_ref, ...), custom_call_target="tpu_custom_call" | custom-call | tf_op jit(solution)/shard_map/convolve_back/pallas_call | solution.py:351
  117.1 20.6 %attend_back.1 = (f32[512,512]{1,0:T(8,128)S(1)}, f32[8,512]{1,0:T(8,128)S(1)}, f32[512,128]{1,0:T(8,128)S(1)}, bf16[16,64,512]{2,1,0:T(8,128)(2,1)S(1)}, bf16[16,64,512]{2,1,0:T(8,128)(2,1)S(1)}) custom-call(s32[3]{0:T(128)S(1)} %pad_add_fusion.place_ref, f32[512,512]{1,0:T(8,128)S(1)} %get-tuple-element.215.grad_ref, f32[512,512]{1,0:T(8,128)S(1)} %ffn_first_down.1.x_ref, ...), custom_call_target="tpu_custom_call" | custom-call | tf_op jit(solution)/shard_map/attend_back/pallas_call | solution.py:351
  142.8 4.5 %ffn_first_out.1 = (bf16[512,2048]{1,0:T(8,128)(2,1)S(1)}, bf16[16,64,512]{2,1,0:T(8,128)(2,1)S(1)}, bf16[16,64,512]{2,1,0:T(8,128)(2,1)S(1)}) custom-call(s32[3]{0:T(128)S(1)} %pad_add_fusion.place_ref, f32[512,512]{1,0:T(8,128)S(1)} %get-tuple-element.226.grad_ref, bf16[512,2048]{1,0:T(8,128)(2,1)S(1)} %get-tuple-element.182.hidden_ref, ...), custom_call_target="tpu_custom_call" | custom-call | tf_op jit(solution)/shard_map/ffn_first_out/pallas_call | solution.py:351
  150.2 4.1 %collective-permute-done.16 = bf16[4,128,512]{2,1,0:T(8,128)(2,1)S(1)} collective-permute-done((bf16[4,128,512]{2,1,0:T(8,128)(2,1)S(1)}, bf16[4,128,512]{2,1,0:T(8,128)(2,1)S(1)}, u32[]{:S(2)}, u32[]{:S(2)}) %collective-permute-start.16) | collective-permute-done | bytes 524320 | tf_op jit(solution)/shard_map/ppermute | solution.py:119
  156.2 5.9 %ffn_first_in.1 = (bf16[512,512]{1,0:T(8,128)(2,1)}, f32[8,512]{1,0:T(8,128)S(1)}, bf16[16,64,512]{2,1,0:T(8,128)(2,1)S(1)}, bf16[16,64,512]{2,1,0:T(8,128)(2,1)S(1)}) custom-call(s32[3]{0:T(128)S(1)} %pad_add_fusion.place_ref, f32[512,512]{1,0:T(8,128)S(1)} %get-tuple-element.226.grad_ref, bf16[512,512]{1,0:T(8,128)(2,1)S(1)} %bitcast.55, ...), custom_call_target="tpu_custom_call" | custom-call | tf_op jit(solution)/shard_map/ffn_first_in/pallas_call | solution.py:351
  164.5 2.6 collective-permute-start.23
  168.6 5.0 %collective-permute-done.23 = bf16[1,128,512]{2,1,0:T(8,128)(2,1)S(1)} collective-permute-done((bf16[1,128,512]{2,1,0:T(8,128)(2,1)S(1)}, bf16[1,128,512]{2,1,0:T(8,128)(2,1)S(1)}, u32[]{:S(2)}, u32[]{:S(2)}) %collective-permute-start.23) | collective-permute-done | bytes 131104 | tf_op jit(solution)/shard_map/ppermute | solution.py:119
  178.9 2.6 collective-permute-start.27
  182.1 2.3 collective-permute-done.30
  187.8 7.3 %collective-permute-done.29 = bf16[8,64,512]{2,1,0:T(8,128)(2,1)S(1)} collective-permute-done((bf16[8,64,512]{2,1,0:T(8,128)(2,1)S(1)}, bf16[8,64,512]{2,1,0:T(8,128)(2,1)S(1)}, u32[]{:S(2)}, u32[]{:S(2)}) %collective-permute-start.29) | collective-permute-done | bytes 524320 | tf_op jit(solution)/shard_map/ppermute | solution.py:119
  198.2 13.1 %collective-permute-done.34 = f32[56,512]{1,0:T(8,128)S(1)} collective-permute-done((f32[56,512]{1,0:T(8,128)S(1)}, f32[56,512]{1,0:T(8,128)S(1)}, u32[]{:S(2)}, u32[]{:S(2)}) %collective-permute-start.34) | collective-permute-done | bytes 114720 | tf_op jit(solution)/shard_map/ppermute | solution.py:119
  214.9 4.9 %collective-permute-done.38 = f32[56,512]{1,0:T(8,128)S(1)} collective-permute-done((f32[56,512]{1,0:T(8,128)S(1)}, f32[56,512]{1,0:T(8,128)S(1)}, u32[]{:S(2)}, u32[]{:S(2)}) %collective-permute-start.38) | collective-permute-done | bytes 114720 | tf_op jit(solution)/shard_map/ppermute | solution.py:119
  226.0 2.7 collective-permute-start.47
  235.6 4.3 %collective-permute-done.40 = bf16[1,128,512]{2,1,0:T(8,128)(2,1)S(1)} collective-permute-done((bf16[1,128,512]{2,1,0:T(8,128)(2,1)S(1)}, bf16[1,128,512]{2,1,0:T(8,128)(2,1)S(1)}, u32[]{:S(2)}, u32[]{:S(2)}) %collective-permute-start.40) | collective-permute-done | bytes 131104 | tf_op jit(solution)/shard_map/ppermute | solution.py:119
  243.6 10.2 %update_out1.1 = (f32[2,1024,512]{2,1,0:T(8,128)}, f32[2,1024,512]{2,1,0:T(8,128)}, f32[2,1024,512]{2,1,0:T(8,128)}, f32[2,1024,512]{2,1,0:T(8,128)}, f32[8,128]{1,0:T(8,128)}) custom-call(s32[16]{0:T(128)} %broadcast_xor_fusion.spot_ref, bf16[8,128,512]{2,1,0:T(8,128)(2,1)} %copy-done.32, bf16[8,128,512]{2,1,0:T(8,128)(2,1)} %copy-done.34, ...), custom_call_target="tpu_custom_call" | custom-call | tf_op jit(solution)/shard_map/update_out1/pallas_call | solution.py:927
  256.2 10.3 %update_in1.1 = (f32[2,256,2048]{2,1,0:T(8,128)}, f32[2,256,2048]{2,1,0:T(8,128)}, f32[2,256,2048]{2,1,0:T(8,128)}, f32[2,256,2048]{2,1,0:T(8,128)}, f32[8,128]{1,0:T(8,128)}) custom-call(s32[16]{0:T(128)} %broadcast_xor_fusion.spot_ref, bf16[8,128,512]{2,1,0:T(8,128)(2,1)} %copy-done.32, bf16[8,128,512]{2,1,0:T(8,128)(2,1)} %copy-done.34, ...), custom_call_target="tpu_custom_call" | custom-call | tf_op jit(solution)/shard_map/update_in1/pallas_call | solution.py:927
  276.6 14.8 %update_rest.1 = (f32[4,256,512]{2,1,0:T(8,128)}, f32[4,256,512]{2,1,0:T(8,128)}, f32[4,256,512]{2,1,0:T(8,128)}, f32[3,256,512]{2,1,0:T(8,128)}, f32[256,512]{1...) custom-call(s32[16]{0:T(128)} %broadcast_xor_fusion.spot_ref, ...), custom_call_target="tpu_custom_call" | custom-call | tf_op jit(solution)/shard_map/update_rest/pallas_call | solution.py:1072
  296.8 5.7 %move_layer.2 = (f32[2,256,2048]{2,1,0:T(8,128)}, f32[2,1024,512]{2,1,0:T(8,128)}) custom-call(f32[2]{0:T(128)} %bitcast.57, f32[2,256,2048]{2,1,0:T(8,128)} %w0.4, f32[2,256,2048]{2,1,0:T(8,128)} %get-tuple-element.282.u0, f32[2,1024,512]{2,1,0:T(8,128)} %w1.4, f32[2,1024,512]{2,1,0:T(8,128)} %get-tuple-element.283.u1), custom_call_target="tpu_custom_call", output_to_operand_aliasing={{0}: (2, {}), {1}: (4, {})} | custom-call | tf_op jit(solution)/shard_map/move_layer/pallas_call | solution.py:955
  304.2 5.3 %move_rest.1 = (f32[4,256,512]{2,1,0:T(8,128)}, f32[256,1536]{1,0:T(8,128)}) custom-call(f32[6]{0:T(128)} %get-tuple-element.420.factor_ref, f32[4,256,512]{2,1,0:T(8,128)} %w0.5, f32[4,256,512]{2,1,0:T(8,128)} %get-tuple-element.306.u0, f32[256,1536]{1,0:T(8,128)} %w1.5, ...), custom_call_target="tpu_custom_call", output_to_operand_aliasing={{0}: (2, {}), {1}: (4, {})} | custom-call | tf_op jit(solution)/shard_map/move_rest/pallas_call | solution.py:979
  311.9 10.2 %update_out0.1 = (f32[2,1024,512]{2,1,0:T(8,128)}, f32[2,1024,512]{2,1,0:T(8,128)}, f32[2,1024,512]{2,1,0:T(8,128)}, f32[2,1024,512]{2,1,0:T(8,128)}, f32[8,128]{1,0:T(8,128)}) custom-call(s32[16]{0:T(128)} %broadcast_xor_fusion.spot_ref, bf16[8,128,512]{2,1,0:T(8,128)(2,1)} %copy-done.33, ...), custom_call_target="tpu_custom_call", output_to_operand_aliasing={{0}: (8, {}), {1}: (9, {}), {2}: (10, {}), {3}: (11, {})} | custom-call | tf_op jit(solution)/shard_map/update_out0/pallas_call | solution.py:927
  322.8 10.3 %update_in0.1 = (f32[2,256,2048]{2,1,0:T(8,128)}, f32[2,256,2048]{2,1,0:T(8,128)}, f32[2,256,2048]{2,1,0:T(8,128)}, f32[2,256,2048]{2,1,0:T(8,128)}, f32[8,128]{1,0:T(8,128)}) custom-call(s32[16]{0:T(128)} %broadcast_xor_fusion.spot_ref, bf16[8,128,512]{2,1,0:T(8,128)(2,1)} %copy-done.33, ...), custom_call_target="tpu_custom_call", output_to_operand_aliasing={{0}: (8, {}), {1}: (9, {}), {2}: (10, {}), {3}: (11, {})} | custom-call | tf_op jit(solution)/shard_map/update_in0/pallas_call | solution.py:927
  342.2 5.7 %move_layer.3 = (f32[2,256,2048]{2,1,0:T(8,128)}, f32[2,1024,512]{2,1,0:T(8,128)}) custom-call(f32[2]{0:T(128)} %get-tuple-element.414.factor_ref, f32[2,256,2048]{2,1,0:T(8,128)} %w0.4, f32[2,256,2048]{2,1,0:T(8,128)} %get-tuple-element.296.u0, f32[2,1024,512]{2,1,0:T(8,128)} %w1.4, ...), custom_call_target="tpu_custom_call", output_to_operand_aliasing={{0}: (2, {}), {1}: (4, {})} | custom-call | tf_op jit(solution)/shard_map/move_layer/pallas_call | solution.py:955
  (292 shorter events, 112.5 us)
Async XLA Ops:
  3.4 17.6 %collective-permute-start.1 = (bf16[128,2048]{1,0:T(8,128)(2,1)}, bf16[128,2048]{1,0:T(8,128)(2,1)}, u32[]{:S(2)}, u32[]{:S(2)}) collective-permute-start(bf16[128,2048]{1,0:T(8,128)(2,1)} %bitcast.66), channel_id=1, source_target_pairs={{0,1},{1,0},{2,3},{3,2},{4,5},{5,4},{6,7},{7,6},{8,9},{9,8},{10,11... | collective-permute-start | bytes 1572872 | tf_op jit(solution)/shard_map/ppermute | solution.py:119
  6.4 14.6 %collective-permute-start = (bf16[37,256]{1,0:T(8,128)(2,1)S(1)}, bf16[37,256]{1,0:T(8,128)(2,1)S(1)}, u32[]{:S(2)}, u32[]{:S(2)}) collective-permute-start(bf16[37,256]{1,0:T(8,128)(2,1)S(1)} %convert_element_type.322), channel_id=1, source_target_pairs={{0,1},{1,0},{2,3},{3,2},{4,5},{5,4},{6,7},{7,6},{8,9},{9,8},{10,11... | collective-permute-start | bytes 56840 | tf_op jit(solution)/shard_map/ppermute | solution.py:119
  21.1 14.9 %collective-permute-start.3 = (bf16[512,512]{1,0:T(8,128)(2,1)}, bf16[512,512]{1,0:T(8,128)(2,1)}, u32[]{:S(2)}, u32[]{:S(2)}) collective-permute-start(bf16[512,512]{1,0:T(8,128)(2,1)} %bitcast.65), channel_id=1, source_target_pairs={{0,1},{1,0},{2,3},{3,2},{4,5},{5,4},{6,7},{7,6},{8,9},{9,8},{10,11... | collective-permute-start | bytes 1572872 | tf_op jit(solution)/shard_map/ppermute | solution.py:119
  35.9 13.7 %collective-permute-start.4 = (bf16[4,128,512]{2,1,0:T(8,128)(2,1)S(1)}, bf16[4,128,512]{2,1,0:T(8,128)(2,1)}, u32[]{:S(2)}, u32[]{:S(2)}) collective-permute-start(bf16[4,128,512]{2,1,0:T(8,128)(2,1)S(1)} %copy-done.30), channel_id=1, source_target_pairs={{0,1},{1,0},{2,3},{3,2},{4,5},{5,4},{6,7},{7,6},{8,9},{9,8},{10,11... | collective-permute-start | bytes 1572872 | tf_op jit(solution)/shard_map/ppermute | solution.py:119
  37.7 15.2 %collective-permute-start.5 = (bf16[512,512]{1,0:T(8,128)(2,1)}, bf16[512,512]{1,0:T(8,128)(2,1)}, u32[]{:S(2)}, u32[]{:S(2)}) collective-permute-start(bf16[512,512]{1,0:T(8,128)(2,1)} %collective-permute-done.3.rest_1_), channel_id=1, source_target_pairs={{0,2},{2,0},{4,6},{6,4},{8,10},{10,8},{12,14},{14,12},{16,18},{18,... | collective-permute-start | bytes 1572872 | tf_op jit(solution)/shard_map/ppermute | solution.py:119
  50.5 20.5 %collective-permute-start.7 = (bf16[128,1536]{1,0:T(8,128)(2,1)}, bf16[128,1536]{1,0:T(8,128)(2,1)S(1)}, u32[]{:S(2)}, u32[]{:S(2)}) collective-permute-start(bf16[128,1536]{1,0:T(8,128)(2,1)} %copy-done.31), channel_id=1, source_target_pairs={{0,1},{1,0},{2,3},{3,2},{4,5},{5,4},{6,7},{7,6},{8,9},{9,8},{10,11... | collective-permute-start | bytes 1179656 | tf_op jit(solution)/shard_map/ppermute | solution.py:119
  52.3 25.9 %collective-permute-start.9 = (bf16[128,2048]{1,0:T(8,128)(2,1)}, bf16[128,2048]{1,0:T(8,128)(2,1)S(1)}, u32[]{:S(2)}, u32[]{:S(2)}) collective-permute-start(bf16[128,2048]{1,0:T(8,128)(2,1)} %copy-done.28), channel_id=1, source_target_pairs={{0,1},{1,0},{2,3},{3,2},{4,5},{5,4},{6,7},{7,6},{8,9},{9,8},{10,11... | collective-permute-start | bytes 1572872 | tf_op jit(solution)/shard_map/ppermute | solution.py:119
  69.4 15.4 %collective-permute-start.11 = (bf16[512,512]{1,0:T(8,128)(2,1)S(1)}, bf16[512,512]{1,0:T(8,128)(2,1)S(1)}, u32[]{:S(2)}, u32[]{:S(2)}) collective-permute-start(bf16[512,512]{1,0:T(8,128)(2,1)S(1)} %copy-done.27), channel_id=1, source_target_pairs={{0,1},{1,0},{2,3},{3,2},{4,5},{5,4},{6,7},{7,6},{8,9},{9,8},{10,11... | collective-permute-start | bytes 1572872 | tf_op jit(solution)/shard_map/ppermute | solution.py:119
  99.1 15.7 %collective-permute-start.13 = (bf16[16,128,512]{2,1,0:T(8,128)(2,1)S(1)}, bf16[16,128,512]{2,1,0:T(8,128)(2,1)S(1)}, u32[]{:S(2)}, u32[]{:S(2)}) collective-permute-start(bf16[16,128,512]{2,1,0:T(8,128)(2,1)S(1)} %get-tuple-element.203), channel_id=1, source_target_pairs={{0,2},{2,0},{4,6},{6,4},{8,10},{10,8},{12,14},{14,12},{16,18},{18,... | collective-permute-start | bytes 6291464 | tf_op jit(solution)/shard_map/ppermute | solution.py:119
  114.4 23.4 %collective-permute-start.15 = (bf16[16,48,512]{2,1,0:T(8,128)(2,1)S(1)}, bf16[16,48,512]{2,1,0:T(8,128)(2,1)S(1)}, u32[]{:S(2)}, u32[]{:S(2)}) collective-permute-start(bf16[16,48,512]{2,1,0:T(8,128)(2,1)S(1)} %get-tuple-element.214), channel_id=1, source_target_pairs={{0,2},{2,0},{4,6},{6,4},{8,10},{10,8},{12,14},{14,12},{16,18},{18,... | collective-permute-start | bytes 2359304 | tf_op jit(solution)/shard_map/ppermute | solution.py:119
  115.6 25.3 %collective-permute-start.14 = (bf16[8,128,512]{2,1,0:T(8,128)(2,1)S(1)}, bf16[8,128,512]{2,1,0:T(8,128)(2,1)S(1)}, u32[]{:S(2)}, u32[]{:S(2)}) collective-permute-start(bf16[8,128,512]{2,1,0:T(8,128)(2,1)S(1)} %get-tuple-element.381), channel_id=1, source_target_pairs={{0,1},{1,0},{2,3},{3,2},{4,5},{5,4},{6,7},{7,6},{8,9},{9,8},{10,11... | collective-permute-start | bytes 3145736 | tf_op jit(solution)/shard_map/ppermute | solution.py:119
  138.1 12.0 %collective-permute-start.18 = (bf16[8,48,512]{2,1,0:T(8,128)(2,1)S(1)}, bf16[8,48,512]{2,1,0:T(8,128)(2,1)S(1)}, u32[]{:S(2)}, u32[]{:S(2)}) collective-permute-start(bf16[8,48,512]{2,1,0:T(8,128)(2,1)S(1)} %get-tuple-element.391), channel_id=1, source_target_pairs={{0,1},{1,0},{2,3},{3,2},{4,5},{5,4},{6,7},{7,6},{8,9},{9,8},{10,11... | collective-permute-start | bytes 1179656 | tf_op jit(solution)/shard_map/ppermute | solution.py:119
  141.2 13.2 %collective-permute-start.16 = (bf16[4,128,512]{2,1,0:T(8,128)(2,1)S(1)}, bf16[4,128,512]{2,1,0:T(8,128)(2,1)S(1)}, u32[]{:S(2)}, u32[]{:S(2)}) collective-permute-start(bf16[4,128,512]{2,1,0:T(8,128)(2,1)S(1)} %get-tuple-element.389), channel_id=1, source_target_pairs={{0,4},{2,6},{4,0},{6,2},{8,12},{10,14},{12,8},{14,10},{16,20},{18,... | collective-permute-start | bytes 1572872 | tf_op jit(solution)/shard_map/ppermute | solution.py:119
  147.6 14.6 %collective-permute-start.19 = (bf16[8,64,512]{2,1,0:T(8,128)(2,1)S(1)}, bf16[8,64,512]{2,1,0:T(8,128)(2,1)S(1)}, u32[]{:S(2)}, u32[]{:S(2)}) collective-permute-start(bf16[8,64,512]{2,1,0:T(8,128)(2,1)S(1)} %get-tuple-element.387), channel_id=1, source_target_pairs={{0,1},{1,0},{2,3},{3,2},{4,5},{5,4},{6,7},{7,6},{8,9},{9,8},{10,11... | collective-permute-start | bytes 1572872 | tf_op jit(solution)/shard_map/ppermute | solution.py:119
  149.8 12.8 %collective-permute-start.21 = (bf16[16,64,512]{2,1,0:T(8,128)(2,1)S(1)}, bf16[16,64,512]{2,1,0:T(8,128)(2,1)S(1)}, u32[]{:S(2)}, u32[]{:S(2)}) collective-permute-start(bf16[16,64,512]{2,1,0:T(8,128)(2,1)S(1)} %get-tuple-element.232), channel_id=1, source_target_pairs={{0,2},{2,0},{4,6},{6,4},{8,10},{10,8},{12,14},{14,12},{16,18},{18,... | collective-permute-start | bytes 3145736 | tf_op jit(solution)/shard_map/ppermute | solution.py:119
  162.9 13.1 %collective-permute-start.24 = (bf16[16,64,512]{2,1,0:T(8,128)(2,1)S(1)}, bf16[16,64,512]{2,1,0:T(8,128)(2,1)S(1)}, u32[]{:S(2)}, u32[]{:S(2)}) collective-permute-start(bf16[16,64,512]{2,1,0:T(8,128)(2,1)S(1)} %get-tuple-element.248), channel_id=1, source_target_pairs={{0,2},{2,0},{4,6},{6,4},{8,10},{10,8},{12,14},{14,12},{16,18},{18,... | collective-permute-start | bytes 3145736 | tf_op jit(solution)/shard_map/ppermute | solution.py:119
  162.9 12.9 %collective-permute-start.22 = (bf16[4,112,512]{2,1,0:T(8,128)(2,1)S(1)}, bf16[4,112,512]{2,1,0:T(8,128)(2,1)S(1)}, u32[]{:S(2)}, u32[]{:S(2)}) collective-permute-start(bf16[4,112,512]{2,1,0:T(8,128)(2,1)S(1)} %pad_maximum_fusion.3), channel_id=1, source_target_pairs={{0,4},{2,6},{4,0},{6,2},{8,12},{10,14},{12,8},{14,10},{16,20},{18,... | collective-permute-start | bytes 1376264 | tf_op jit(solution)/shard_map/ppermute | solution.py:119
  167.1 14.8 %collective-permute-start.28 = (bf16[8,64,512]{2,1,0:T(8,128)(2,1)S(1)}, bf16[8,64,512]{2,1,0:T(8,128)(2,1)S(1)}, u32[]{:S(2)}, u32[]{:S(2)}) collective-permute-start(bf16[8,64,512]{2,1,0:T(8,128)(2,1)S(1)} %get-tuple-element.252), channel_id=1, source_target_pairs={{0,1},{1,0},{2,3},{3,2},{4,5},{5,4},{6,7},{7,6},{8,9},{9,8},{10,11... | collective-permute-start | bytes 1572872 | tf_op jit(solution)/shard_map/ppermute | solution.py:119
  177.9 17.3 %collective-permute-start.29 = (bf16[8,64,512]{2,1,0:T(8,128)(2,1)S(1)}, bf16[8,64,512]{2,1,0:T(8,128)(2,1)S(1)}, u32[]{:S(2)}, u32[]{:S(2)}) collective-permute-start(bf16[8,64,512]{2,1,0:T(8,128)(2,1)S(1)} %get-tuple-element.253), channel_id=1, source_target_pairs={{0,1},{1,0},{2,3},{3,2},{4,5},{5,4},{6,7},{7,6},{8,9},{9,8},{10,11... | collective-permute-start | bytes 1572872 | tf_op jit(solution)/shard_map/ppermute | solution.py:119
  195.3 16.2 %collective-permute-start.33 = (bf16[4,128,512]{2,1,0:T(8,128)(2,1)S(1)}, bf16[4,128,512]{2,1,0:T(8,128)(2,1)S(1)}, u32[]{:S(2)}, u32[]{:S(2)}) collective-permute-start(bf16[4,128,512]{2,1,0:T(8,128)(2,1)S(1)} %pad_maximum_fusion.1), channel_id=1, source_target_pairs={{0,4},{2,6},{4,0},{6,2},{8,12},{10,14},{12,8},{14,10},{16,20},{18,... | collective-permute-start | bytes 1572872 | tf_op jit(solution)/shard_map/ppermute | solution.py:119
  195.9 15.4 %collective-permute-start.34 = (f32[56,512]{1,0:T(8,128)S(1)}, f32[56,512]{1,0:T(8,128)S(1)}, u32[]{:S(2)}, u32[]{:S(2)}) collective-permute-start(f32[56,512]{1,0:T(8,128)S(1)} %add.245), channel_id=1, source_target_pairs={{0,4},{2,6},{4,0},{6,2},{8,12},{10,14},{12,8},{14,10},{16,20},{18,... | collective-permute-start | bytes 344072 | tf_op jit(solution)/shard_map/ppermute | solution.py:119
  197.4 13.9 %collective-permute-start.31 = (bf16[1,112,512]{2,1,0:T(8,128)(2,1)S(1)}, bf16[1,112,512]{2,1,0:T(8,128)(2,1)S(1)}, u32[]{:S(2)}, u32[]{:S(2)}) collective-permute-start(bf16[1,112,512]{2,1,0:T(8,128)(2,1)S(1)} %add_convert_fusion.33), channel_id=1, source_target_pairs={{0,16},{2,18},{4,20},{6,22},{8,24},{10,26},{12,28},{14,30},{16,0},... | collective-permute-start | bytes 344072 | tf_op jit(solution)/shard_map/ppermute | solution.py:119
  197.7 13.7 %collective-permute-start.32 = (bf16[2,128,512]{2,1,0:T(8,128)(2,1)S(1)}, bf16[2,128,512]{2,1,0:T(8,128)(2,1)S(1)}, u32[]{:S(2)}, u32[]{:S(2)}) collective-permute-start(bf16[2,128,512]{2,1,0:T(8,128)(2,1)S(1)} %pad_maximum_fusion.6), channel_id=1, source_target_pairs={{0,8},{2,10},{4,12},{6,14},{8,0},{10,2},{12,4},{14,6},{16,24},{18,... | collective-permute-start | bytes 786440 | tf_op jit(solution)/shard_map/ppermute | solution.py:119
  212.2 11.5 %collective-permute-start.37 = (bf16[2,128,512]{2,1,0:T(8,128)(2,1)S(1)}, bf16[2,128,512]{2,1,0:T(8,128)(2,1)S(1)}, u32[]{:S(2)}, u32[]{:S(2)}) collective-permute-start(bf16[2,128,512]{2,1,0:T(8,128)(2,1)S(1)} %get-tuple-element.261), channel_id=1, source_target_pairs={{0,8},{2,10},{4,12},{6,14},{8,0},{10,2},{12,4},{14,6},{16,24},{18,... | collective-permute-start | bytes 786440 | tf_op jit(solution)/shard_map/ppermute | solution.py:119
  213.8 12.1 %collective-permute-start.36 = (bf16[4,128,512]{2,1,0:T(8,128)(2,1)S(1)}, bf16[4,128,512]{2,1,0:T(8,128)(2,1)S(1)}, u32[]{:S(2)}, u32[]{:S(2)}) collective-permute-start(bf16[4,128,512]{2,1,0:T(8,128)(2,1)S(1)} %pad_maximum_fusion.2), channel_id=1, source_target_pairs={{0,4},{2,6},{4,0},{6,2},{8,12},{10,14},{12,8},{14,10},{16,20},{18,... | collective-permute-start | bytes 1572872 | tf_op jit(solution)/shard_map/ppermute | solution.py:119
  230.2 12.4 %collective-permute-start.41 = (bf16[8,128,512]{2,1,0:T(8,128)(2,1)S(1)}, bf16[8,128,512]{2,1,0:T(8,128)(2,1)S(1)}, u32[]{:S(2)}, u32[]{:S(2)}) collective-permute-start(bf16[8,128,512]{2,1,0:T(8,128)(2,1)S(1)} %pad_maximum_fusion.g0_near.g1_near), channel_id=1, source_target_pairs={{0,2},{2,0},{4,6},{6,4},{8,10},{10,8},{12,14},{14,12},{16,18},{18,... | collective-permute-start | bytes 3145736 | tf_op jit(solution)/shard_map/ppermute | solution.py:119
  240.0 13.8 %collective-permute-start.43 = (bf16[1,128,512]{2,1,0:T(8,128)(2,1)S(1)}, bf16[1,128,512]{2,1,0:T(8,128)(2,1)S(1)}, u32[]{:S(2)}, u32[]{:S(2)}) collective-permute-start(bf16[1,128,512]{2,1,0:T(8,128)(2,1)S(1)} %add_convert_fusion.26), channel_id=1, source_target_pairs={{0,16},{2,18},{4,20},{6,22},{8,24},{10,26},{12,28},{14,30},{16,0},... | collective-permute-start | bytes 393224 | tf_op jit(solution)/shard_map/ppermute | solution.py:119
  241.4 13.1 %collective-permute-start.42 = (bf16[4,112,512]{2,1,0:T(8,128)(2,1)S(1)}, bf16[4,112,512]{2,1,0:T(8,128)(2,1)S(1)}, u32[]{:S(2)}, u32[]{:S(2)}) collective-permute-start(bf16[4,112,512]{2,1,0:T(8,128)(2,1)S(1)} %pad_maximum_fusion.4), channel_id=1, source_target_pairs={{0,4},{2,6},{4,0},{6,2},{8,12},{10,14},{12,8},{14,10},{16,20},{18,... | collective-permute-start | bytes 1376264 | tf_op jit(solution)/shard_map/ppermute | solution.py:119
  253.8 12.7 %collective-permute-start.44 = (bf16[2,128,512]{2,1,0:T(8,128)(2,1)S(1)}, bf16[2,128,512]{2,1,0:T(8,128)(2,1)}, u32[]{:S(2)}, u32[]{:S(2)}) collective-permute-start(bf16[2,128,512]{2,1,0:T(8,128)(2,1)S(1)} %constant_dynamic-update-slice_fusion.2), channel_id=1, source_target_pairs={{0,8},{2,10},{4,12},{6,14},{8,0},{10,2},{12,4},{14,6},{16,24},{18,... | collective-permute-start | bytes 786440 | tf_op jit(solution)/shard_map/ppermute | solution.py:119
  254.6 21.1 %collective-permute-start.45 = (bf16[8,112,512]{2,1,0:T(8,128)(2,1)S(1)}, bf16[8,112,512]{2,1,0:T(8,128)(2,1)S(1)}, u32[]{:S(2)}, u32[]{:S(2)}) collective-permute-start(bf16[8,112,512]{2,1,0:T(8,128)(2,1)S(1)} %constant_dynamic-update-slice_fusion.g0_near.g1_near), channel_id=1, source_target_pairs={{0,2},{2,0},{4,6},{6,4},{8,10},{10,8},{12,14},{14,12},{16,18},{18,... | collective-permute-start | bytes 2752520 | tf_op jit(solution)/shard_map/ppermute | solution.py:119
  267.5 23.9 %collective-permute-start.46 = (bf16[4,128,512]{2,1,0:T(8,128)(2,1)S(1)}, bf16[4,128,512]{2,1,0:T(8,128)(2,1)S(1)}, u32[]{:S(2)}, u32[]{:S(2)}) collective-permute-start(bf16[4,128,512]{2,1,0:T(8,128)(2,1)S(1)} %constant_dynamic-update-slice_fusion.4), channel_id=1, source_target_pairs={{0,4},{2,6},{4,0},{6,2},{8,12},{10,14},{12,8},{14,10},{16,20},{18,... | collective-permute-start | bytes 1572872 | tf_op jit(solution)/shard_map/ppermute | solution.py:119
  291.5 19.4 %collective-permute-start.49 = (bf16[8,128,512]{2,1,0:T(8,128)(2,1)S(1)}, bf16[8,128,512]{2,1,0:T(8,128)(2,1)S(1)}, u32[]{:S(2)}, u32[]{:S(2)}) collective-permute-start(bf16[8,128,512]{2,1,0:T(8,128)(2,1)S(1)} %constant_dynamic-update-slice_fusion.6.g0_near.g1_near), channel_id=1, source_target_pairs={{0,2},{2,0},{4,6},{6,4},{8,10},{10,8},{12,14},{14,12},{16,18},{18,... | collective-permute-start | bytes 3145736 | tf_op jit(solution)/shard_map/ppermute | solution.py:119
  (68 other events, 454.4 us)
